TPU v7x, 512 devices: a whole 4x4x16 slice. The times are simulated.
512 devices in a mesh: wide: 64 (over z, y_hi, core), narrow: 8 (over y_lo, x).
Axes of the slice: x: 4, y: 4 (y_hi: 2, y_lo: 2; y = y_hi * 2 + y_lo), z: 16, core: 2. Of those that a mesh axis runs over, the one named last changes fastest.
Arguments:
- offsets: float32 [3, 64, 8, 512], P(None, 'wide', 'narrow'), may hold values from 0 to 1
- bases: int32 [3, 64, 8, 512], P(None, 'wide', 'narrow'), may hold values from 0 to 511, as said below
- charges: float32 [64, 8, 512], P('wide', 'narrow'), may hold values from -4 to 4
- counts: int32 [64, 8], P('wide', 'narrow'), may hold values from 32 to 512, as said below
- cotangent: float32 [1], replicated, may hold values from 0.5 to 2
Outputs:
- forces: float32 [3, 64, 8, 512], P(None, 'wide', 'narrow')
- charge_grads: float32 [64, 8, 512], P('wide', 'narrow')
Inputs may be any that keep to these rules, and one draw needn't show every extreme that they name: `counts`: slots at or beyond a domain's count are padding; some domain holds exactly 512 atoms. `bases`: component 0 is below 4 and component 1 below 8 (the lowest stencil cell lies in the atom's own domain); component 2 is below 512.
All inputs are finite; a program needn't handle non-finite values.
Results may differ from a plain program's by a relative error of at most 0.0003.
Values sent between devices are 32-bit elements; how exact they have to be, the bound alone decides.
A program may use at most 64 MiB of HBM per device.

v0:
```python
import math

import jax
import jax.numpy as jnp
from jax import lax
from jax.sharding import PartitionSpec as P

CX = 4
CY = 8
NZ = 512


PRECISE = lax.Precision.HIGHEST
splitting_width = 1.0
block_limit = 512


def from_behind(block, axis, distance):
    devices = range(lax.axis_size(axis))
    route = [((i - distance) % len(devices), i) for i in devices]
    return lax.ppermute(block, axis, route)


def spline_pair(offset):
    rest = 1.0 - offset
    square = offset * offset
    cube = square * offset
    weights = jnp.stack(
        [
            rest * rest * rest / 6.0,
            (3.0 * cube - 6.0 * square + 4.0) / 6.0,
            (-3.0 * cube + 3.0 * square + 3.0 * offset + 1.0) / 6.0,
            cube / 6.0,
        ],
        axis=1,
    )
    slopes = jnp.stack(
        [
            -0.5 * rest * rest,
            1.5 * square - 2.0 * offset,
            -1.5 * square + offset + 0.5,
            0.5 * square,
        ],
        axis=1,
    )
    return (weights, slopes)


def wave_terms(wave_index, length):
    signed = (
        jnp.where(2 * wave_index < length, wave_index, wave_index - length).astype(jnp.float32)
        / length
    )
    phase_angle = (wave_index % length).astype(jnp.float32) * (2.0 * math.pi / length)
    spline = 9.0 / (2.0 + jnp.cos(phase_angle)) ** 2
    return (signed * signed, spline)


def influence(wave_x, wave_y, wave_z, size_x, size_y, size_z):
    square_x, spline_x = wave_terms(wave_x, size_x)
    square_y, spline_y = wave_terms(wave_y, size_y)
    square_z, spline_z = wave_terms(wave_z, size_z)
    squared = square_x + square_y + square_z
    positive = jnp.where(squared > 0.0, squared, 1.0)
    volume = float(size_x * size_y * size_z)
    kernel = jnp.exp(-math.pi**2 * squared / (splitting_width * splitting_width)) / (
        math.pi * volume * positive
    )
    kernel = kernel * spline_x * spline_y * spline_z
    return jnp.where(squared > 0.0, kernel, 0.0)


def dft_tables(length, sign):
    wave = jnp.arange(length, dtype=jnp.int32)
    phase = wave[:, None] * wave[None, :] % length
    phase_angle = phase.astype(jnp.float32) * (2.0 * math.pi / length)
    return (jnp.cos(phase_angle), sign * jnp.sin(phase_angle))


def rotation_matrix(width):
    row_ids = jnp.arange(width, dtype=jnp.int32)[:, None]
    column_ids = jnp.arange(width, dtype=jnp.int32)[None, :]
    raise_part = ((row_ids % 2 == 0) & (column_ids == row_ids + 1)).astype(jnp.float32)
    lower_part = ((row_ids % 2 == 1) & (column_ids == row_ids - 1)).astype(jnp.float32)
    return raise_part - lower_part


def complex_dft(values, cosine_table, sine_table, rotation, einsum_form):
    real_term = jnp.einsum(einsum_form, cosine_table, values, precision=PRECISE)
    turned = jnp.einsum(einsum_form, sine_table, values, precision=PRECISE)
    return real_term + jnp.dot(turned, rotation, precision=PRECISE)


def axis_table(cells, corner_row, values, wrap):
    cell_ids = jnp.arange(cells, dtype=jnp.int32)[:, None]
    table = jnp.zeros((cells, corner_row.shape[0]), jnp.float32)
    for step_index in range(4):
        target = corner_row + step_index
        if wrap:
            target = target % cells
        table = table + jnp.where(cell_ids == target[None, :], values[step_index][None, :], 0.0)
    return table


def spread_atoms(running, fraction, corner, charge, ext_rows, depth):
    ext_planes = running.shape[0] // (ext_rows * depth)
    weights = spline_pair(fraction)[0]
    plane_table = axis_table(ext_planes, corner[0], weights[0], False)
    row_table = axis_table(ext_rows, corner[1], weights[1], False)
    depth_table = axis_table(depth, corner[2], weights[2], True)
    cross = (plane_table[:, None, :] * row_table[None, :, :] * charge[None, None, :]).reshape(
        ext_planes * ext_rows, -1
    )
    grid = lax.dot_general(cross, depth_table, (((1,), (1,)), ((), ())), precision=PRECISE)
    return running + grid.reshape(-1)


def interpolate(fraction, corner, charge, occupied, potential_flat, ext_rows, depth, factor):
    ext_planes = potential_flat.shape[0] // (ext_rows * depth)
    weights, slopes = spline_pair(fraction)
    plane_w = axis_table(ext_planes, corner[0], weights[0], False)
    plane_s = axis_table(ext_planes, corner[0], slopes[0], False)
    row_w = axis_table(ext_rows, corner[1], weights[1], False)
    row_s = axis_table(ext_rows, corner[1], slopes[1], False)
    depth_w = axis_table(depth, corner[2], weights[2], True)
    depth_s = axis_table(depth, corner[2], slopes[2], True)
    potential_grid = potential_flat.reshape(ext_planes * ext_rows, depth)
    along_w = jnp.dot(potential_grid, depth_w, precision=PRECISE).reshape(ext_planes, ext_rows, -1)
    along_s = jnp.dot(potential_grid, depth_s, precision=PRECISE).reshape(ext_planes, ext_rows, -1)
    rows_ww = jnp.sum(row_w[None, :, :] * along_w, axis=1)
    rows_sw = jnp.sum(row_s[None, :, :] * along_w, axis=1)
    rows_ws = jnp.sum(row_w[None, :, :] * along_s, axis=1)
    potential_sum = jnp.sum(plane_w * rows_ww, axis=0)
    pull_x = jnp.sum(plane_s * rows_ww, axis=0)
    pull_y = jnp.sum(plane_w * rows_sw, axis=0)
    pull_z = jnp.sum(plane_w * rows_ws, axis=0)
    grads = factor * occupied * potential_sum
    pulls = -factor * charge[None] * jnp.stack([pull_x, pull_y, pull_z])
    return (grads, pulls)


def on_device(offsets, bases, charges, counts, cotangent):
    wide_count = lax.axis_size("wide")
    narrow_count = lax.axis_size("narrow")
    slots = charges.shape[2]
    ext_planes = CX + 3
    ext_rows = CY + 3
    grid_x = CX * wide_count
    grid_y = CY * narrow_count
    row_share = grid_y // wide_count
    fraction = offsets[:, 0, 0, :]
    corner = bases[:, 0, 0, :]
    occupied = (jnp.arange(slots, dtype=jnp.int32) < counts[0, 0]).astype(jnp.float32)
    charge = charges[0, 0] * occupied
    factor = cotangent[0]
    size_block = math.gcd(slots, block_limit)
    cell_count = ext_planes * ext_rows * NZ

    def spread_all(block_index, running):
        return spread_atoms(running, fraction, corner, charge, ext_rows, NZ)

    flat_grid = lax.fori_loop(
        0, slots // size_block, spread_all, jnp.zeros((cell_count,), jnp.float32)
    )
    charge_grid = flat_grid.reshape(ext_planes, ext_rows, NZ)
    z_cosine, z_sine = dft_tables(NZ, -1.0)
    forward_z = jnp.stack([z_cosine, z_sine], axis=2).reshape(NZ, 2 * NZ)
    inverse_z = jnp.stack([z_cosine, z_sine], axis=1).reshape(2 * NZ, NZ)
    spectrum_width = 2 * NZ
    length = spectrum_width // narrow_count
    freq_share = length // 2
    rotation = rotation_matrix(length)
    y_cosine, y_sine = dft_tables(grid_y, -1.0)
    x_cosine, x_sine = dft_tables(grid_x, -1.0)
    planes_in = from_behind(charge_grid[CX:], "wide", 1)
    charge_grid = charge_grid[:CX].at[:3].add(planes_in)
    rows_in = from_behind(charge_grid[:, CY:], "narrow", 1)
    charge_grid = charge_grid[:, :CY].at[:, :3].add(rows_in)
    z_spectrum = jnp.dot(charge_grid.reshape(CX * CY, NZ), forward_z, precision=PRECISE).reshape(
        CX, CY, spectrum_width
    )
    columns = lax.all_to_all(z_spectrum, "narrow", split_axis=2, concat_axis=1, tiled=True)
    columns = complex_dft(columns, y_cosine, y_sine, rotation, "kn,pnl->pkl")
    spectrum = lax.all_to_all(columns, "wide", split_axis=1, concat_axis=0, tiled=True)
    spectrum = complex_dft(spectrum, x_cosine, x_sine, rotation, "kn,nrl->krl")
    wave_x = jnp.arange(grid_x, dtype=jnp.int32)[:, None, None]
    wave_y = (
        lax.axis_index("wide") * row_share + jnp.arange(row_share, dtype=jnp.int32)[None, :, None]
    )
    wave_z = (
        lax.axis_index("narrow") * freq_share
        + jnp.arange(freq_share, dtype=jnp.int32)[None, None, :]
    )
    kernel = influence(wave_x, wave_y, wave_z, grid_x, grid_y, NZ)
    filtered = spectrum * jnp.repeat(kernel, 2, axis=2)
    spectrum = complex_dft(filtered, x_cosine, -x_sine, rotation, "kn,nrl->krl")
    columns = lax.all_to_all(spectrum, "wide", split_axis=0, concat_axis=1, tiled=True)
    columns = complex_dft(columns, y_cosine, -y_sine, rotation, "kn,pnl->pkl")
    returned = lax.all_to_all(columns, "narrow", split_axis=1, concat_axis=2, tiled=True)
    potential = jnp.dot(
        returned.reshape(CX * CY, spectrum_width), inverse_z, precision=PRECISE
    ).reshape(CX, CY, NZ)
    upper_planes = from_behind(potential[:3], "wide", -1)
    potential = jnp.concatenate([potential, upper_planes], axis=0)
    side_rows = from_behind(potential[:, :3], "narrow", -1)
    potential = jnp.concatenate([potential, side_rows], axis=1)
    potential_flat = potential.reshape(-1)

    def read_block(block_index, results):
        grads_part, pulls_part = interpolate(
            fraction, corner, charge, occupied, potential_flat, ext_rows, NZ, factor
        )
        return (grads_part, pulls_part)

    start_results = (jnp.zeros((slots,), jnp.float32), jnp.zeros((3, slots), jnp.float32))
    grads, pulls = lax.fori_loop(0, slots // size_block, read_block, start_results)
    return (pulls.reshape(3, 1, 1, slots), grads.reshape(1, 1, slots))


def solution(mesh):
    placed = (
        P(None, "wide", "narrow", None),
        P(None, "wide", "narrow", None),
        P("wide", "narrow", None),
        P("wide", "narrow"),
        P(),
    )
    return jax.shard_map(
        on_device,
        mesh=mesh,
        in_specs=placed,
        out_specs=(P(None, "wide", "narrow", None), P("wide", "narrow", None)),
        check_vma=False,
    )
```

profile of v0, /device:TPU:1, one launch (start us, length us, event | category | flops | bytes accessed | tf_op | source)
XLA Modules:
  0.0 146.2 jit_solution(6606350430928284395)
XLA Ops:
  5.2 6.2 %collective-permute-start = (f32[3,11,512]{2,1,0:T(8,128)S(1)}, f32[3,11,512]{2,1,0:T(8,128)S(1)}, u32[]{:S(2)}, u32[]{:S(2)}) collective-permute-start(f32[3,11,512]{2,1,0:T(8,128)S(1)} %slice.335), channel_id=1, source_target_pairs={{504,0},{0,8},{8,16},{16,24},{24,32},{32,40},{40,48},{48,56},{56,6... | collective-permute-start | bytes 202760 | tf_op jit(solution)/shard_map/ppermute | solution.py:21
  11.4 5.3 %sine_multiply_fusion.1 = (f32[512,512,1]{1,0,2:T(8,128)S(1)}, f32[512,512,1]{1,0,2:T(8,128)}) fusion(), kind=kLoop, calls=%fused_computation.40 | loop fusion | flops 3932160 | bytes 2097152 | tf_op jit(solution)/shard_map/mul | solution.py:77
  16.8 3.1 %collective-permute-start.1 = (f32[4,3,512]{2,1,0:T(4,128)S(1)}, f32[4,3,512]{2,1,0:T(4,128)S(1)}, u32[]{:S(2)}, u32[]{:S(2)}) collective-permute-start(f32[4,3,512]{2,1,0:T(4,128)S(1)} %slice.371), channel_id=1, source_target_pairs={{7,0},{0,1},{1,2},{2,3},{3,4},{4,5},{5,6},{6,7},{15,8},{8,9},{9,10... | collective-permute-start | bytes 73736 | tf_op jit(solution)/shard_map/ppermute | solution.py:21
  21.4 2.5 %copy.38 = f32[512,512,2]{0,2,1:T(2,128)} copy(f32[512,512,2]{1,0,2:T(8,128)S(1)} %pad_maximum_fusion) | data formatting | bytes 4194304 | tf_op jit(solution)/shard_map/stack | solution.py:167
  23.8 2.7 %reshape.1289 = f32[512,1024]{0,1:T(8,128)S(1)} reshape(f32[512,512,2]{0,2,1:T(2,128)} %copy.38) | data formatting | bytes 4194304 | tf_op jit(solution)/shard_map/reshape | solution.py:167
  26.8 2.0 %fusion = f32[4,8,1024]{2,1,0:T(8,128)S(1)} fusion(f32[4,8,512]{2,1,0:T(8,128)S(1)} %scatter-add.9, f32[512,1024]{0,1:T(8,128)S(1)} %reshape.1289), kind=kOutput, calls=%fused_computation.2 | convolution fusion | flops 201326592 | bytes 2293760 | tf_op jit(solution)/shard_map/dot_general | solution.py:179
  29.6 3.1 %reshape.1301 = f32[8,1,4096]{2,1,0:T(1,128)} reshape(f32[1024,4,8]{2,1,0:T(4,128)S(1)} %bitcast.169) | data formatting | bytes 262144
  32.7 3.8 %all-to-all-start = ((f32[8,1,4096]{2,1,0:T(1,128)}), f32[8,1,4096]{2,1,0:T(1,128)S(1)}, u32[]{:S(2)}, u32[]{:S(2)}) async-start(f32[8,1,4096]{2,1,0:T(1,128)} %reshape.1301), calls=%async_computation | async-start | bytes 262144 | tf_op jit(solution)/shard_map/all_to_all | solution.py:182
  36.6 5.4 %all-to-all-done = f32[8,1,4096]{2,1,0:T(1,128)S(1)} async-done(((f32[8,1,4096]{2,1,0:T(1,128)}), f32[8,1,4096]{2,1,0:T(1,128)S(1)}, u32[]{:S(2)}, u32[]{:S(2)}) %all-to-all-start) | async-done | bytes 131104 | tf_op jit(solution)/shard_map/all_to_all | solution.py:182
  43.4 2.5 %reshape.1302 = f32[1024,4,8]{2,1,0:T(4,128)S(1)} reshape(f32[8,4096]{1,0:T(8,128)S(1)} %reduce.4) | data formatting | bytes 262144
  48.6 18.5 %all-to-all-start.1 = ((f32[4,64,128]{2,0,1:T(4,128)}), f32[4,64,128]{2,0,1:T(4,128)S(1)}, u32[]{:S(2)}, u32[]{:S(2)}) async-start(f32[4,64,128]{2,0,1:T(4,128)} %copy.42), calls=%async_computation.1 | async-start | bytes 262144 | tf_op jit(solution)/shard_map/all_to_all | solution.py:184
  67.8 18.0 %all-to-all-done.1 = f32[4,64,128]{2,0,1:T(4,128)S(1)} async-done(((f32[4,64,128]{2,0,1:T(4,128)}), f32[4,64,128]{2,0,1:T(4,128)S(1)}, u32[]{:S(2)}, u32[]{:S(2)}) %all-to-all-start.1) | async-done | bytes 131104 | tf_op jit(solution)/shard_map/all_to_all | solution.py:184
  87.7 1.6 %fusion.2 = f32[256,128]{1,0:T(8,128)S(1)} fusion(f32[256,128]{1,0:T(8,128)S(1)} %copy.43, f32[256,128]{1,0:T(8,128)S(1)} %fusion.93, f32[256,128]{1,0:T(8,128)S(1)} %bitcast.179), kind=kOutput, calls=%fused_computation.13 | convolution fusion | flops 101646336 | bytes 524288 | tf_op jit(solution)/shard_map/kn,nrl->krl/dot_general | solution.py:89
  89.3 1.6 %fusion.59 = f32[256,128]{1,0:T(8,128)S(1)} fusion(f32[256,128]{1,0:T(8,128)S(1)} %fusion.2), kind=kOutput, calls=%fused_computation.86 | convolution fusion | flops 101711872 | bytes 262144 | tf_op jit(solution)/shard_map/kn,nrl->krl/dot_general | solution.py:90
  91.2 2.0 %convolution_add_fusion = f32[256,128]{1,0:T(8,128)} fusion(f32[256,128]{1,0:T(8,128)S(1)} %fusion.92, f32[256,128]{1,0:T(8,128)S(1)} %fusion.2), kind=kOutput, calls=%fused_computation.11 | convolution fusion | flops 101613568 | bytes 393216 | tf_op jit(solution)/shard_map/kn,nrl->krl/dot_general | solution.py:89
  93.2 4.4 %all-to-all-start.2 = ((f32[256,1,128]{2,1,0:T(1,128)}), f32[256,1,128]{2,1,0:T(1,128)S(1)}, u32[]{:S(2)}, u32[]{:S(2)}) async-start(f32[256,1,128]{2,1,0:T(1,128)} %bitcast.43), calls=%async_computation.2 | async-start | bytes 262144 | tf_op jit(solution)/shard_map/all_to_all | solution.py:197
  97.7 4.1 %sine_multiply_fusion = (f32[512,1,512]{2,0,1:T(8,128)S(1)}, f32[512,1,512]{2,0,1:T(8,128)S(1)}) fusion(), kind=kLoop, calls=%fused_computation.37 | loop fusion | flops 3932160 | bytes 2097152 | tf_op jit(solution)/shard_map/mul | solution.py:77
  101.8 14.6 %all-to-all-done.2 = f32[256,1,128]{2,1,0:T(1,128)S(1)} async-done(((f32[256,1,128]{2,1,0:T(1,128)}), f32[256,1,128]{2,1,0:T(1,128)S(1)}, u32[]{:S(2)}, u32[]{:S(2)}) %all-to-all-start.2) | async-done | bytes 131104 | tf_op jit(solution)/shard_map/all_to_all | solution.py:197
  118.3 3.6 %all-to-all-start.3 = ((f32[4,64,128]{2,0,1:T(4,128)}), f32[4,64,128]{2,0,1:T(4,128)S(1)}, u32[]{:S(2)}, u32[]{:S(2)}) async-start(f32[4,64,128]{2,0,1:T(4,128)} %copy.46), calls=%async_computation.3 | async-start | bytes 262144 | tf_op jit(solution)/shard_map/all_to_all | solution.py:199
  122.1 3.0 %copy.48 = f32[512,2,512]{2,1,0:T(2,128)} copy(f32[512,2,512]{2,0,1:T(8,128)S(1)} %pad_maximum_fusion.1) | data formatting | bytes 4194304 | tf_op jit(solution)/shard_map/stack | solution.py:168
  125.0 2.7 %reshape.1292 = f32[1024,512]{1,0:T(8,128)S(1)} reshape(f32[512,2,512]{2,1,0:T(2,128)} %copy.48) | data formatting | bytes 4194304 | tf_op jit(solution)/shard_map/reshape | solution.py:168
  129.2 2.7 %collective-permute-start.2 = (f32[3,8,512]{2,1,0:T(8,128)S(1)}, f32[3,8,512]{2,1,0:T(8,128)S(1)}, u32[]{:S(2)}, u32[]{:S(2)}) collective-permute-start(f32[3,8,512]{2,1,0:T(8,128)S(1)} %slice_bitcast_fusion), channel_id=1, source_target_pairs={{8,0},{16,8},{24,16},{32,24},{40,32},{48,40},{56,48},{64,56},{72,6... | collective-permute-start | bytes 147464 | tf_op jit(solution)/shard_map/ppermute | solution.py:21
  132.6 3.5 %collective-permute-done.2 = f32[3,8,512]{2,1,0:T(8,128)S(1)} collective-permute-done((f32[3,8,512]{2,1,0:T(8,128)S(1)}, f32[3,8,512]{2,1,0:T(8,128)S(1)}, u32[]{:S(2)}, u32[]{:S(2)}) %collective-permute-start.2) | collective-permute-done | bytes 49184 | tf_op jit(solution)/shard_map/ppermute | solution.py:21
  136.1 5.2 %collective-permute-start.3 = (f32[7,3,512]{2,1,0:T(4,128)S(1)}, f32[7,3,512]{2,1,0:T(4,128)S(1)}, u32[]{:S(2)}, u32[]{:S(2)}) collective-permute-start(f32[7,3,512]{2,1,0:T(4,128)S(1)} %pad_maximum_fusion.5), channel_id=1, source_target_pairs={{1,0},{2,1},{3,2},{4,3},{5,4},{6,5},{7,6},{0,7},{9,8},{10,9},{11,1... | collective-permute-start | bytes 129032 | tf_op jit(solution)/shard_map/ppermute | solution.py:21
  (66 shorter events, 21.6 us)
Async XLA Ops:
  5.2 11.6 %collective-permute-start = (f32[3,11,512]{2,1,0:T(8,128)S(1)}, f32[3,11,512]{2,1,0:T(8,128)S(1)}, u32[]{:S(2)}, u32[]{:S(2)}) collective-permute-start(f32[3,11,512]{2,1,0:T(8,128)S(1)} %slice.335), channel_id=1, source_target_pairs={{504,0},{0,8},{8,16},{16,24},{24,32},{32,40},{40,48},{48,56},{56,6... | collective-permute-start | bytes 202760 | tf_op jit(solution)/shard_map/ppermute | solution.py:21
  16.8 9.7 %collective-permute-start.1 = (f32[4,3,512]{2,1,0:T(4,128)S(1)}, f32[4,3,512]{2,1,0:T(4,128)S(1)}, u32[]{:S(2)}, u32[]{:S(2)}) collective-permute-start(f32[4,3,512]{2,1,0:T(4,128)S(1)} %slice.371), channel_id=1, source_target_pairs={{7,0},{0,1},{1,2},{2,3},{3,4},{4,5},{5,6},{6,7},{15,8},{8,9},{9,10... | collective-permute-start | bytes 73736 | tf_op jit(solution)/shard_map/ppermute | solution.py:21
  32.7 9.3 %all-to-all-start = ((f32[8,1,4096]{2,1,0:T(1,128)}), f32[8,1,4096]{2,1,0:T(1,128)S(1)}, u32[]{:S(2)}, u32[]{:S(2)}) async-start(f32[8,1,4096]{2,1,0:T(1,128)} %reshape.1301), calls=%async_computation | async-start | bytes 262144 | tf_op jit(solution)/shard_map/all_to_all | solution.py:182
  48.6 37.1 %all-to-all-start.1 = ((f32[4,64,128]{2,0,1:T(4,128)}), f32[4,64,128]{2,0,1:T(4,128)S(1)}, u32[]{:S(2)}, u32[]{:S(2)}) async-start(f32[4,64,128]{2,0,1:T(4,128)} %copy.42), calls=%async_computation.1 | async-start | bytes 262144 | tf_op jit(solution)/shard_map/all_to_all | solution.py:184
  93.2 23.1 %all-to-all-start.2 = ((f32[256,1,128]{2,1,0:T(1,128)}), f32[256,1,128]{2,1,0:T(1,128)S(1)}, u32[]{:S(2)}, u32[]{:S(2)}) async-start(f32[256,1,128]{2,1,0:T(1,128)} %bitcast.43), calls=%async_computation.2 | async-start | bytes 262144 | tf_op jit(solution)/shard_map/all_to_all | solution.py:197
  118.3 9.5 %all-to-all-start.3 = ((f32[4,64,128]{2,0,1:T(4,128)}), f32[4,64,128]{2,0,1:T(4,128)S(1)}, u32[]{:S(2)}, u32[]{:S(2)}) async-start(f32[4,64,128]{2,0,1:T(4,128)} %copy.46), calls=%async_computation.3 | async-start | bytes 262144 | tf_op jit(solution)/shard_map/all_to_all | solution.py:199
  127.7 13.6 %copy-start = (f32[1,1,512]{2,1,0:T(1,128)S(1)}, f32[1,1,512]{2,1,0:T(1,128)}, u32[]{:S(2)}) copy-start(f32[1,1,512]{2,1,0:T(1,128)} %param.11) | copy-start | bytes 6148
  129.2 6.9 %collective-permute-start.2 = (f32[3,8,512]{2,1,0:T(8,128)S(1)}, f32[3,8,512]{2,1,0:T(8,128)S(1)}, u32[]{:S(2)}, u32[]{:S(2)}) collective-permute-start(f32[3,8,512]{2,1,0:T(8,128)S(1)} %slice_bitcast_fusion), channel_id=1, source_target_pairs={{8,0},{16,8},{24,16},{32,24},{40,32},{48,40},{56,48},{64,56},{72,6... | collective-permute-start | bytes 147464 | tf_op jit(solution)/shard_map/ppermute | solution.py:21
  136.1 6.4 %collective-permute-start.3 = (f32[7,3,512]{2,1,0:T(4,128)S(1)}, f32[7,3,512]{2,1,0:T(4,128)S(1)}, u32[]{:S(2)}, u32[]{:S(2)}) collective-permute-start(f32[7,3,512]{2,1,0:T(4,128)S(1)} %pad_maximum_fusion.5), channel_id=1, source_target_pairs={{1,0},{2,1},{3,2},{4,3},{5,4},{6,5},{7,6},{0,7},{9,8},{10,9},{11,1... | collective-permute-start | bytes 129032 | tf_op jit(solution)/shard_map/ppermute | solution.py:21
where the time goes:
time: 147 us; the launch traced here: 146 us
  starting transfers between devices  47.6 us (32%)
  waiting for transfers between devices  42.7 us (29%)
  local copies, waits for them, and re-layouts  21.3 us (14%)
  matrix products  17.1 us (12%)
  other arithmetic  15 us (10%)
  between operations  2.55 us (2%)
    all_to_all x1, starting transfers between devices, on_device(): lax.all_to_all(columns, 'wide', split_axis=1, concat_axis=0, tiled=True)  18.5 us
    all_to_all x1, waiting for transfers between devices, on_device(): lax.all_to_all(columns, 'wide', split_axis=1, concat_axis=0, tiled=True)  18 us
    ppermute x4, starting transfers between devices, from_behind(): return lax.ppermute(block, axis, route)  17.2 us
    all_to_all x1, waiting for transfers between devices, on_device(): lax.all_to_all(spectrum, 'wide', split_axis=0, concat_axis=1, tiled=True)  14.6 us
    mul x2, other arithmetic, dft_tables(): return (jnp.cos(phase_angle), sign * jnp.sin(phase_angle))  9.43 us
    unnamed x4, local copies, waits for them, and re-layouts  5.56 us
    all_to_all x1, waiting for transfers between devices, on_device(): lax.all_to_all(z_spectrum, 'narrow', split_axis=2, concat_axis=1, tiled=T...  5.42 us
    ppermute x4, waiting for transfers between devices, from_behind(): return lax.ppermute(block, axis, route)  4.74 us
  transfers between devices with their start and end apart: 8, of which 5 were waited for; matrix products, arithmetic and copies ran while one was open for 15% of the time, Pallas kernels for 0%

commit v1 on v0

v1 whole, which is shorter than its diff:
```python
import math

import jax
import jax.numpy as jnp
import ml_dtypes
import numpy as np
from jax import lax
from jax.experimental import pallas as pl
from jax.experimental.pallas import tpu as pltpu
from jax.sharding import PartitionSpec as P

CX = 4
CY = 8
NZ = 512
WIDE = 64
NARROW = 8
NX = CX * WIDE
NY = CY * NARROW
SLOTS = 512
ROWS = 24
HALF = 64
MESH = pl.DeviceIdType.MESH
VMEM = pltpu.VMEM
F32 = jnp.float32
BF16 = jnp.bfloat16


def real_basis(length):
    c = np.arange(length)
    freq = np.where(c <= length // 2, c, length - c)
    phase = (freq[:, None] * c[None, :]) % length * (2.0 * np.pi / length)
    scale = np.where((freq == 0) | (2 * freq == length), 1.0, np.sqrt(2.0)) / np.sqrt(length)
    table = np.where((c <= length // 2)[:, None], np.cos(phase), np.sin(phase)) * scale[:, None]
    return table, freq


def halves(table):
    table = np.asarray(table, np.float32)
    high = table.astype(ml_dtypes.bfloat16)
    low = (table - high.astype(np.float32)).astype(ml_dtypes.bfloat16)
    return high, low


def frequency_factors(length):
    freq = real_basis(length)[1]
    square = (freq / length) ** 2
    spline = 9.0 / (2.0 + np.cos(2.0 * np.pi * freq / length)) ** 2
    return square, np.exp(-(np.pi**2) * square) * spline


def row_matrix():
    basis = real_basis(NY)[0]
    i = np.arange(ROWS)
    row = np.where(i < 16, i % 8, 8 + i % 4)
    parity = np.where(i < 16, i // 8, (i // 4) % 2)
    table = np.zeros((NARROW, ROWS, 2, NY))
    for n in range(NARROW):
        for j in range(ROWS):
            if row[j] < CY + 3:
                table[n, j, parity[j]] = basis[:, (CY * n + row[j]) % NY]
    return table.reshape(NARROW * ROWS, 2 * NY)


def split(value):
    high = value.astype(BF16)
    return high, (value - high.astype(F32)).astype(BF16)


def dot3(a, b, contract):
    dims = (contract, ((), ()))

    def one(x, y):
        return lax.dot_general(x, y, dims, preferred_element_type=F32)

    return one(a[0], b[0]) + (one(a[0], b[1]) + one(a[1], b[0]))


def pick(steps, values):
    out = jnp.where(steps == 3, values[3], 0.0)
    for j in (2, 1, 0):
        out = jnp.where(steps == j, values[j], out)
    return out


def spline_weights(t):
    s = 1.0 - t
    square = t * t
    cube = square * t
    return (
        s * s * s / 6.0,
        (3.0 * cube - 6.0 * square + 4.0) / 6.0,
        (-3.0 * cube + 3.0 * square + 3.0 * t + 1.0) / 6.0,
        cube / 6.0,
    )


def spline_slopes(t):
    s = 1.0 - t
    square = t * t
    return (-0.5 * s * s, 1.5 * square - 2.0 * t, -1.5 * square + t + 0.5, 0.5 * square)


def swap(value):
    return pltpu.roll(value, HALF, 1)


def kernel(
    count_ref,
    factor_ref,
    zsquare_ref,
    zgain_ref,
    offset_ref,
    base_ref,
    charge_ref,
    zh_ref,
    zl_ref,
    yh_ref,
    yl_ref,
    yth_ref,
    ytl_ref,
    xh_ref,
    xl_ref,
    xth_ref,
    xtl_ref,
    gain_ref,
    square_ref,
    force_ref,
    grad_ref,
    send_a,
    recv_a,
    send_b,
    recv_b,
    send_c,
    recv_c,
    send_d,
    recv_d,
    depth_h,
    depth_l,
    slope_h,
    slope_l,
    send_sems,
    recv_sems,
):
    w = lax.axis_index("wide")
    n = lax.axis_index("narrow")
    above = lax.rem(w + 1, WIDE)
    below = lax.rem(w + WIDE - 1, WIDE)

    barrier = pltpu.get_barrier_semaphore()

    def greet(to):
        pl.semaphore_signal(barrier, inc=1, device_id=to, device_id_type=MESH)

    def greet_wide(i, carry):
        greet((lax.rem(w + i, WIDE), n))
        return carry

    def greet_narrow(i, carry):
        other = lax.rem(n + i, NARROW)
        greet((w, other))
        greet((above, other))
        greet((below, other))
        return carry

    lax.fori_loop(1, NARROW, greet_narrow, 0)
    lax.fori_loop(1, WIDE, greet_wide, 0)

    low_lanes = lax.broadcasted_iota(jnp.int32, (1, 128), 1) < HALF

    t = [offset_ref[d : d + 1, :] for d in range(3)]
    corner = [base_ref[d : d + 1, :] for d in range(3)]
    weights = [spline_weights(v) for v in t]
    slopes = [spline_slopes(v) for v in t]
    occupied = lax.broadcasted_iota(jnp.int32, (1, SLOTS), 1) < count_ref[0, 0]
    charge = jnp.where(occupied, charge_ref[...], 0.0)

    def depth_steps(first):
        cell = lax.broadcasted_iota(jnp.int32, (128, SLOTS), 0) + first
        return (cell - corner[2]) & (NZ - 1)

    for first in range(0, NZ, 128):
        high, low = split(pick(depth_steps(first), weights[2]))
        depth_h[first : first + 128, :] = high
        depth_l[first : first + 128, :] = low

    index = lax.broadcasted_iota(jnp.int32, (ROWS, SLOTS), 0)
    row = jnp.where(index < 16, index & 7, 8 + (index & 3))
    parity = jnp.where(index < 16, index >> 3, (index >> 2) & 1)
    row_steps = row - corner[1]
    row_w = pick(row_steps, weights[1])
    row_s = pick(row_steps, slopes[1])
    plane_steps = [parity + 2 * g - corner[0] for g in range(4)]
    row_q = row_w * charge
    cross = jnp.concatenate([row_q * pick(plane_steps[g], weights[0]) for g in range(4)], axis=0)
    grid = dot3(split(cross), (depth_h[...], depth_l[...]), ((1,), (1,)))
    spectrum = dot3(split(grid), (zh_ref[...], zl_ref[...]), ((1,), (0,)))
    for side in range(2):
        for m in range(4):
            lanes = slice(128 * m, 128 * m + 128)
            first = spectrum[ROWS * 2 * side : ROWS * (2 * side + 1), lanes]
            second = spectrum[ROWS * (2 * side + 1) : ROWS * (2 * side + 2), lanes]
            send_a[8 * side + 2 * m] = jnp.where(low_lanes, first, swap(second))
            send_a[8 * side + 2 * m + 1] = jnp.where(low_lanes, swap(first), second)

    pl.semaphore_wait(barrier, 3 * (NARROW - 1) + WIDE - 1)

    def push(stage, source, target, to):
        pltpu.make_async_remote_copy(
            src_ref=source,
            dst_ref=target,
            send_sem=send_sems.at[stage],
            recv_sem=recv_sems.at[stage],
            device_id=to,
            device_id_type=MESH,
        ).start()

    def drain(stage, block):
        return pltpu.make_async_remote_copy(
            src_ref=block,
            dst_ref=block,
            send_sem=send_sems.at[stage],
            recv_sem=recv_sems.at[stage],
            device_id=(w, n),
            device_id_type=MESH,
        )

    def push_a(i, carry):
        other = lax.rem(n + i, NARROW)
        push(0, send_a.at[other], recv_a.at[n], (w, other))
        push(0, send_a.at[8 + other], recv_a.at[8 + n], (above, other))
        return carry

    push(0, send_a.at[8 + n], recv_a.at[8 + n], (above, n))
    lax.fori_loop(1, NARROW, push_a, 0)
    recv_a[n] = send_a[n]

    for first in range(0, NZ, 128):
        high, low = split(pick(depth_steps(first), slopes[2]))
        slope_h[first : first + 128, :] = high
        slope_l[first : first + 128, :] = low
    coefficient = HALF * n + w
    squared = square_ref[...] + zsquare_ref[0, coefficient]
    positive = jnp.where(squared > 0.0, squared, 1.0)
    influence = jnp.where(squared > 0.0, gain_ref[...] * zgain_ref[0, coefficient] / positive, 0.0)

    drain(0, recv_a.at[pl.ds(0, 15)]).wait_recv()
    rows = recv_a[0:8] + recv_a[8:16]
    rows = rows.reshape(NARROW * ROWS, 128)
    columns = dot3((yth_ref[...], ytl_ref[...]), split(rows), ((1,), (0,)))
    columns = columns.T
    send_b[pl.ds(0, HALF, 2), :] = columns[:HALF]
    send_b[pl.ds(1, HALF, 2), :] = columns[HALF:]

    def push_b(i, carry):
        other = lax.rem(w + i, WIDE)
        push(1, send_b.at[pl.ds(2 * other, 2)], recv_b.at[pl.ds(2 * w, 2)], (other, n))
        return carry

    lax.fori_loop(1, WIDE, push_b, 0)
    recv_b[pl.ds(2 * w, 2), :] = send_b[pl.ds(2 * w, 2), :]
    drain(1, recv_b.at[pl.ds(0, 2 * WIDE - 2)]).wait_recv()

    planes = recv_b[...]
    turned = swap(planes)
    stacked = jnp.concatenate(
        [jnp.where(low_lanes, planes, turned), jnp.where(low_lanes, turned, planes)], axis=0
    )
    filtered = dot3((xh_ref[...], xl_ref[...]), split(stacked), ((1,), (0,))) * influence
    planes = dot3((xth_ref[...], xtl_ref[...]), split(filtered), ((1,), (0,)))
    send_c[...] = jnp.where(low_lanes, planes[:128], planes[128:])

    def push_c(i, carry):
        other = lax.rem(w + i, WIDE)
        push(2, send_c.at[pl.ds(2 * other, 2)], recv_c.at[pl.ds(2 * w, 2)], (other, n))
        return carry

    lax.fori_loop(1, WIDE, push_c, 0)
    recv_c[pl.ds(2 * w, 2), :] = send_c[pl.ds(2 * w, 2), :]
    drain(2, recv_c.at[pl.ds(0, 2 * WIDE - 2)]).wait_recv()

    columns = jnp.concatenate(
        [recv_c[pl.ds(0, HALF, 2), :], recv_c[pl.ds(1, HALF, 2), :]], axis=0
    )
    rows = dot3((yh_ref[...], yl_ref[...]), split(columns), ((1,), (1,)))
    send_d[...] = rows.reshape(NARROW, ROWS, 128)

    def push_d(i, carry):
        other = lax.rem(n + i, NARROW)
        push(3, send_d.at[other], recv_d.at[n], (w, other))
        push(3, send_d.at[other], recv_d.at[8 + n], (below, other))
        return carry

    push(3, send_d.at[n], recv_d.at[8 + n], (below, n))
    lax.fori_loop(1, NARROW, push_d, 0)
    recv_d[n] = send_d[n]
    drain(3, recv_d.at[pl.ds(0, 15)]).wait_recv()

    groups = []
    for side in range(2):
        tiles = [recv_d[8 * side + m] for m in range(8)]
        pairs = [(tiles[2 * m], tiles[2 * m + 1]) for m in range(4)]
        groups.append(jnp.concatenate([jnp.where(low_lanes, a, swap(b)) for a, b in pairs], axis=1))
        groups.append(jnp.concatenate([jnp.where(low_lanes, swap(a), b) for a, b in pairs], axis=1))
    spectrum = jnp.concatenate(groups, axis=0)
    potential = split(dot3(split(spectrum), (zh_ref[...], zl_ref[...]), ((1,), (1,))))
    along_w = dot3(potential, (depth_h[...], depth_l[...]), ((1,), (0,)))
    along_s = dot3(potential, (slope_h[...], slope_l[...]), ((1,), (0,)))

    total = jnp.zeros((ROWS, SLOTS), F32)
    pull_x, pull_y, pull_z = total, total, total
    for g in range(4):
        part = slice(ROWS * g, ROWS * g + ROWS)
        plane_w = pick(plane_steps[g], weights[0])
        plane_s = pick(plane_steps[g], slopes[0])
        weighted = along_w[part] * plane_w
        total = total + weighted
        pull_x = pull_x + along_w[part] * plane_s
        pull_z = pull_z + along_s[part] * plane_w

    def over_rows(value):
        return jnp.sum(value, axis=0, keepdims=True)

    factor = factor_ref[0]
    pull_y = over_rows(total * row_s)
    total = over_rows(total * row_w)
    pull_x = over_rows(pull_x * row_w)
    pull_z = over_rows(pull_z * row_w)
    grad_ref[...] = jnp.where(occupied, factor * total, 0.0)
    pull = -factor * charge
    force_ref[0:1, :] = pull * pull_x
    force_ref[1:2, :] = pull * pull_y
    force_ref[2:3, :] = pull * pull_z

    drain(0, recv_a.at[pl.ds(0, 15)]).wait_send()
    drain(1, recv_b.at[pl.ds(0, 2 * WIDE - 2)]).wait_send()
    drain(2, recv_c.at[pl.ds(0, 2 * WIDE - 2)]).wait_send()
    drain(3, recv_d.at[pl.ds(0, 15)]).wait_send()


def on_device(offsets, bases, charges, counts, cotangent):
    z_table = halves(real_basis(NZ)[0].T)
    y_table = row_matrix()
    y_pair = halves(y_table)
    y_turned = halves(y_table.T)
    x_basis = real_basis(NX)[0]
    x_table = np.concatenate([x_basis[:, 0::2], x_basis[:, 1::2]], axis=1)
    x_pair = halves(x_table)
    x_turned = halves(x_table.T)
    square_x, gain_x = frequency_factors(NX)
    square_y, gain_y = frequency_factors(NY)
    square_z, gain_z = frequency_factors(NZ)
    square = (square_x[:, None] + np.tile(square_y, 2)[None, :]).astype(np.float32)
    gain = (gain_x[:, None] * np.tile(gain_y, 2)[None, :] / math.pi).astype(np.float32)
    scalars = pl.BlockSpec(memory_space=pltpu.SMEM)
    arrays = pl.BlockSpec(memory_space=VMEM)
    forces, grads = pl.pallas_call(
        kernel,
        out_shape=(
            jax.ShapeDtypeStruct((3, SLOTS), F32),
            jax.ShapeDtypeStruct((1, SLOTS), F32),
        ),
        in_specs=[scalars] * 4 + [arrays] * 15,
        out_specs=(arrays, arrays),
        scratch_shapes=[
            VMEM((2 * NARROW, ROWS, 128), F32),
            VMEM((2 * NARROW, ROWS, 128), F32),
            VMEM((2 * WIDE, 128), F32),
            VMEM((2 * WIDE, 128), F32),
            VMEM((2 * WIDE, 128), F32),
            VMEM((2 * WIDE, 128), F32),
            VMEM((NARROW, ROWS, 128), F32),
            VMEM((2 * NARROW, ROWS, 128), F32),
            VMEM((NZ, SLOTS), BF16),
            VMEM((NZ, SLOTS), BF16),
            VMEM((NZ, SLOTS), BF16),
            VMEM((NZ, SLOTS), BF16),
            pltpu.SemaphoreType.DMA((4,)),
            pltpu.SemaphoreType.DMA((4,)),
        ],
        compiler_params=pltpu.CompilerParams(
            collective_id=0, has_side_effects=True, vmem_limit_bytes=40 * 1024 * 1024
        ),
        name="ewald",
    )(
        counts,
        cotangent,
        square_z.astype(np.float32).reshape(1, NZ),
        gain_z.astype(np.float32).reshape(1, NZ),
        offsets.reshape(3, SLOTS),
        bases.reshape(3, SLOTS),
        charges.reshape(1, SLOTS),
        *z_table,
        *y_pair,
        *y_turned,
        *x_pair,
        *x_turned,
        gain,
        square,
    )
    return forces.reshape(3, 1, 1, SLOTS), grads.reshape(1, 1, SLOTS)


def solution(mesh):
    placed = (
        P(None, "wide", "narrow", None),
        P(None, "wide", "narrow", None),
        P("wide", "narrow", None),
        P("wide", "narrow"),
        P(),
    )
    return jax.shard_map(
        on_device,
        mesh=mesh,
        in_specs=placed,
        out_specs=(P(None, "wide", "narrow", None), P("wide", "narrow", None)),
        check_vma=False,
    )
```

time: 147 us -> 70.1 us (0.48)
  Pallas kernels: 0 us -> 54.2 us
  starting transfers between devices: 47.6 us -> 0 us
  waiting for transfers between devices: 42.7 us -> 0 us
  matrix products: 17.1 us -> 0 us
  other arithmetic: 15 us -> 0 us
  local copies, waits for them, and re-layouts: 21.3 us -> 13.4 us
    pallas_call x0 -> x1, Pallas kernels: none -> 54.2 us  [on_device(): pl.pallas_call(kernel, out_shape=(jax.ShapeDtypeStruct((3, SLOTS), F32),...]
    all_to_all x4 -> x0, waiting for transfers between devices: 38 us -> none  [the longest x1 18 us: on_device(): lax.all_to_all(columns, 'wide', split_axis=1, concat_axis=0, tiled=True)]
    all_to_all x4 -> x0, starting transfers between devices: 30.4 us -> none  [the longest x1 18.5 us: on_device(): lax.all_to_all(columns, 'wide', split_axis=1, concat_axis=0, tiled=True)]
    ppermute x4 -> x0, starting transfers between devices: 17.2 us -> none  [from_behind(): return lax.ppermute(block, axis, route)]
    dot_general x17 -> x0, matrix products: 17.1 us -> none  [the longest x4 4.34 us: complex_dft(): real_term = jnp.einsum(einsum_form, cosine_table, values, precision=PRECISE)]
    mul x8 -> x0, other arithmetic: 12.1 us -> none  [the longest x2 9.43 us: dft_tables(): return (jnp.cos(phase_angle), sign * jnp.sin(phase_angle))]
    unnamed x4 -> x36, local copies, waits for them, and re-layouts: 5.56 us -> 13.4 us
    another operation x3 -> x0, local copies, waits for them, and re-layouts: 5.43 us -> none  [the longest x1 2.96 us: on_device(): inverse_z = jnp.stack([z_cosine, z_sine], axis=1).reshape(2 * NZ, NZ)]
  transfers between devices with their start and end apart: 8 -> 0, of which waited for: 5 -> 0; matrix products, arithmetic and copies ran while one was open for 15% -> 0% of each run, Pallas kernels for 0% -> 0%
where the time goes in v1:
time: 70.1 us; the launch traced here: 69.5 us
  Pallas kernels  54.2 us (77%)
  local copies, waits for them, and re-layouts  13.4 us (19%)
  between operations  1.97 us (3%)
    pallas_call x1, Pallas kernels, on_device(): pl.pallas_call(kernel, out_shape=(jax.ShapeDtypeStruct((3, SLOTS), F32),...  54.2 us
    unnamed x36, local copies, waits for them, and re-layouts  13.4 us

profile of v1, /device:TPU:1, one launch (start us, length us, event | category | flops | bytes accessed | tf_op | source)
XLA Modules:
  0.0 69.5 jit_solution(5953686597576143566)
XLA Ops:
  1.9 0.0 copy-start.15
  1.9 0.7 %copy.27 = f32[3,1,1,512]{3,0,1,2:T(4,128)S(1)} copy(f32[3,1,1,512]{3,2,1,0:T(1,128)} %param.19) | data formatting | bytes 12288
  2.6 0.0 copy-done.15
  2.6 0.0 copy-start.12
  2.6 0.0 copy-start.13
  2.6 0.0 copy-start.14
  2.7 0.7 copy-done.12
  3.3 0.0 copy-done.13
  3.3 0.0 copy-done.14
  3.4 1.0 %copy-done = bf16[512,512]{1,0:T(8,128)(2,1)S(1)} copy-done((bf16[512,512]{1,0:T(8,128)(2,1)S(1)}, bf16[512,512]{1,0:T(8,128)(2,1)}, u32[]{:S(2)}) %copy-start) | copy-done | bytes 524312
  4.4 1.0 %copy-done.1 = bf16[512,512]{1,0:T(8,128)(2,1)S(1)} copy-done((bf16[512,512]{1,0:T(8,128)(2,1)S(1)}, bf16[512,512]{1,0:T(8,128)(2,1)}, u32[]{:S(2)}) %copy-start.1) | copy-done | bytes 524312
  5.4 0.9 %copy-done.2 = f32[256,128]{1,0:T(8,128)S(1)} copy-done((f32[256,128]{1,0:T(8,128)S(1)}, f32[256,128]{1,0:T(8,128)}, u32[]{:S(2)}) %copy-start.2) | copy-done | bytes 131096
  6.3 0.9 %copy-done.3 = f32[256,128]{1,0:T(8,128)S(1)} copy-done((f32[256,128]{1,0:T(8,128)S(1)}, f32[256,128]{1,0:T(8,128)}, u32[]{:S(2)}) %copy-start.3) | copy-done | bytes 131096
  7.2 0.9 %copy-done.4 = bf16[256,256]{1,0:T(8,128)(2,1)S(1)} copy-done((bf16[256,256]{1,0:T(8,128)(2,1)S(1)}, bf16[256,256]{1,0:T(8,128)(2,1)}, u32[]{:S(2)}) %copy-start.4) | copy-done | bytes 131096
  8.2 0.9 %copy-done.5 = bf16[256,256]{1,0:T(8,128)(2,1)S(1)} copy-done((bf16[256,256]{1,0:T(8,128)(2,1)S(1)}, bf16[256,256]{1,0:T(8,128)(2,1)}, u32[]{:S(2)}) %copy-start.5) | copy-done | bytes 131096
  9.1 0.9 %copy-done.6 = bf16[256,256]{1,0:T(8,128)(2,1)S(1)} copy-done((bf16[256,256]{1,0:T(8,128)(2,1)S(1)}, bf16[256,256]{1,0:T(8,128)(2,1)}, u32[]{:S(2)}) %copy-start.6) | copy-done | bytes 131096
  10.0 0.9 %copy-done.7 = bf16[256,256]{1,0:T(8,128)(2,1)S(1)} copy-done((bf16[256,256]{1,0:T(8,128)(2,1)S(1)}, bf16[256,256]{1,0:T(8,128)(2,1)}, u32[]{:S(2)}) %copy-start.7) | copy-done | bytes 131096
  10.9 0.8 %copy-done.8 = bf16[128,192]{1,0:T(8,128)(2,1)S(1)} copy-done((bf16[128,192]{1,0:T(8,128)(2,1)S(1)}, bf16[128,192]{1,0:T(8,128)(2,1)}, u32[]{:S(2)}) %copy-start.8) | copy-done | bytes 49176
  11.7 0.8 %copy-done.9 = bf16[128,192]{1,0:T(8,128)(2,1)S(1)} copy-done((bf16[128,192]{1,0:T(8,128)(2,1)S(1)}, bf16[128,192]{1,0:T(8,128)(2,1)}, u32[]{:S(2)}) %copy-start.9) | copy-done | bytes 49176
  12.5 0.8 %copy-done.10 = bf16[192,128]{1,0:T(8,128)(2,1)S(1)} copy-done((bf16[192,128]{1,0:T(8,128)(2,1)S(1)}, bf16[192,128]{1,0:T(8,128)(2,1)}, u32[]{:S(2)}) %copy-start.10) | copy-done | bytes 49176
  13.3 0.8 %copy-done.11 = bf16[192,128]{1,0:T(8,128)(2,1)S(1)} copy-done((bf16[192,128]{1,0:T(8,128)(2,1)S(1)}, bf16[192,128]{1,0:T(8,128)(2,1)}, u32[]{:S(2)}) %copy-start.11) | copy-done | bytes 49176
  14.1 54.2 %ewald.1 = (f32[3,512]{1,0:T(4,128)S(1)}, f32[1,512]{1,0:T(1,128)S(1)}) custom-call(s32[1,1]{1,0:T(1,128)S(6)} %copy.29.count_ref, f32[1]{0:T(128)S(6)} %copy.30.factor_ref, f32[1,512]{1,0:T(1,128)S(1)} %copy-done.14, f32[1,512]{1,0:T(1,128)S(1)} %copy-done.13, f32[3,512]{1,0:T(4,128)S(1)} %bitcast.9, s32[3,512]{1,0:T(4,128)S(1)} %bitcast.10, ...), custom_call_target="tpu_custom_call" | custom-call | tf_op jit(solution)/shard_map/ewald/pallas_call | solution.py:356
  68.3 0.6 copy.21
  68.9 0.6 copy.31
  (13 shorter events, 0.0 us)
Async XLA Ops:
  1.9 0.7 %copy-start.15 = (s32[3,1,1,512]{3,2,1,0:T(1,128)S(1)}, s32[3,1,1,512]{3,2,1,0:T(1,128)}, u32[]{:S(2)}) copy-start(s32[3,1,1,512]{3,2,1,0:T(1,128)} %param.20) | copy-start | bytes 18436
  2.6 0.7 copy-start.12
  2.6 0.7 %copy-start.13 = (f32[1,512]{1,0:T(1,128)S(1)}, f32[1,512]{1,0:T(1,128)}, u32[]{:S(2)}) copy-start(f32[1,512]{1,0:T(1,128)} %constant.29.clone.zgain_ref) | copy-start | bytes 6148
  2.6 0.7 %copy-start.14 = (f32[1,512]{1,0:T(1,128)S(1)}, f32[1,512]{1,0:T(1,128)}, u32[]{:S(2)}) copy-start(f32[1,512]{1,0:T(1,128)} %constant.28.clone.zsquare_ref) | copy-start | bytes 6148
  3.4 1.0 %copy-start = (bf16[512,512]{1,0:T(8,128)(2,1)S(1)}, bf16[512,512]{1,0:T(8,128)(2,1)}, u32[]{:S(2)}) copy-start(bf16[512,512]{1,0:T(8,128)(2,1)} %constant.31.clone.zl_ref) | copy-start | bytes 1572868
  4.4 1.0 %copy-start.1 = (bf16[512,512]{1,0:T(8,128)(2,1)S(1)}, bf16[512,512]{1,0:T(8,128)(2,1)}, u32[]{:S(2)}) copy-start(bf16[512,512]{1,0:T(8,128)(2,1)} %constant.30.clone.zh_ref) | copy-start | bytes 1572868
  5.4 0.9 %copy-start.2 = (f32[256,128]{1,0:T(8,128)S(1)}, f32[256,128]{1,0:T(8,128)}, u32[]{:S(2)}) copy-start(f32[256,128]{1,0:T(8,128)} %constant.41.clone.square_ref) | copy-start | bytes 393220
  6.3 0.9 %copy-start.3 = (f32[256,128]{1,0:T(8,128)S(1)}, f32[256,128]{1,0:T(8,128)}, u32[]{:S(2)}) copy-start(f32[256,128]{1,0:T(8,128)} %constant.40.clone.gain_ref) | copy-start | bytes 393220
  7.2 0.9 %copy-start.4 = (bf16[256,256]{1,0:T(8,128)(2,1)S(1)}, bf16[256,256]{1,0:T(8,128)(2,1)}, u32[]{:S(2)}) copy-start(bf16[256,256]{1,0:T(8,128)(2,1)} %constant.39.clone.xtl_ref) | copy-start | bytes 393220
  8.1 0.9 %copy-start.5 = (bf16[256,256]{1,0:T(8,128)(2,1)S(1)}, bf16[256,256]{1,0:T(8,128)(2,1)}, u32[]{:S(2)}) copy-start(bf16[256,256]{1,0:T(8,128)(2,1)} %constant.38.clone.xth_ref) | copy-start | bytes 393220
  9.1 0.9 %copy-start.6 = (bf16[256,256]{1,0:T(8,128)(2,1)S(1)}, bf16[256,256]{1,0:T(8,128)(2,1)}, u32[]{:S(2)}) copy-start(bf16[256,256]{1,0:T(8,128)(2,1)} %constant.37.clone.xl_ref) | copy-start | bytes 393220
  10.0 0.9 %copy-start.7 = (bf16[256,256]{1,0:T(8,128)(2,1)S(1)}, bf16[256,256]{1,0:T(8,128)(2,1)}, u32[]{:S(2)}) copy-start(bf16[256,256]{1,0:T(8,128)(2,1)} %constant.36.clone.xh_ref) | copy-start | bytes 393220
  10.9 0.8 %copy-start.8 = (bf16[128,192]{1,0:T(8,128)(2,1)S(1)}, bf16[128,192]{1,0:T(8,128)(2,1)}, u32[]{:S(2)}) copy-start(bf16[128,192]{1,0:T(8,128)(2,1)} %constant.35.clone.ytl_ref) | copy-start | bytes 147460
  11.7 0.8 %copy-start.9 = (bf16[128,192]{1,0:T(8,128)(2,1)S(1)}, bf16[128,192]{1,0:T(8,128)(2,1)}, u32[]{:S(2)}) copy-start(bf16[128,192]{1,0:T(8,128)(2,1)} %constant.34.clone.yth_ref) | copy-start | bytes 147460
  12.5 0.8 %copy-start.10 = (bf16[192,128]{1,0:T(8,128)(2,1)S(1)}, bf16[192,128]{1,0:T(8,128)(2,1)}, u32[]{:S(2)}) copy-start(bf16[192,128]{1,0:T(8,128)(2,1)} %constant.33.clone.yl_ref) | copy-start | bytes 147460
  13.3 0.8 %copy-start.11 = (bf16[192,128]{1,0:T(8,128)(2,1)S(1)}, bf16[192,128]{1,0:T(8,128)(2,1)}, u32[]{:S(2)}) copy-start(bf16[192,128]{1,0:T(8,128)(2,1)} %constant.32.clone.yh_ref) | copy-start | bytes 147460

commit v2 on v1

v2 whole, which is shorter than its diff:
```python
import math

import jax
import jax.numpy as jnp
import ml_dtypes
import numpy as np
from jax import lax
from jax.experimental import pallas as pl
from jax.experimental.pallas import tpu as pltpu
from jax.sharding import PartitionSpec as P

CX = 4
CY = 8
NZ = 512
WIDE = 64
NARROW = 8
NX = CX * WIDE
NY = CY * NARROW
SLOTS = 512
ROWS = CY + 3
RING = 16
DOMAINS = WIDE // RING
PLANES = CX + 3
HALF = 64
MESH = pl.DeviceIdType.MESH
VMEM = pltpu.VMEM
F32 = jnp.float32
BF16 = jnp.bfloat16


def real_basis(length):
    c = np.arange(length)
    freq = np.where(c <= length // 2, c, length - c)
    phase = (freq[:, None] * c[None, :]) % length * (2.0 * np.pi / length)
    scale = np.where((freq == 0) | (2 * freq == length), 1.0, np.sqrt(2.0)) / np.sqrt(length)
    table = np.where((c <= length // 2)[:, None], np.cos(phase), np.sin(phase)) * scale[:, None]
    return table, freq


def halves(table):
    table = np.asarray(table, np.float32)
    high = table.astype(ml_dtypes.bfloat16)
    low = (table - high.astype(np.float32)).astype(ml_dtypes.bfloat16)
    return high, low


def frequency_factors(length):
    freq = real_basis(length)[1]
    square = (freq / length) ** 2
    spline = 9.0 / (2.0 + np.cos(2.0 * np.pi * freq / length)) ** 2
    return square, np.exp(-(np.pi**2) * square) * spline


def row_matrix():
    basis = real_basis(NY)[0]
    table = np.zeros((2, NARROW, ROWS, 2, NY))
    for half in range(2):
        for n in range(NARROW):
            for r in range(ROWS):
                table[half, n, r, half] = basis[:, (CY * n + r) % NY]
    return table.reshape(2 * NARROW * ROWS, 2 * NY)


def plane_order():
    half, place, other, plane = np.meshgrid(
        np.arange(2), np.arange(RING), np.arange(2), np.arange(CX), indexing="ij"
    )
    return (CX * (DOMAINS * place + 2 * other + half) + plane).reshape(-1)


def split(value):
    high = value.astype(BF16)
    return high, (value - high.astype(F32)).astype(BF16)


def dot3(a, b, contract):
    dims = (contract, ((), ()))

    def one(x, y):
        return lax.dot_general(x, y, dims, preferred_element_type=F32)

    return one(a[0], b[0]) + (one(a[0], b[1]) + one(a[1], b[0]))


def pick(steps, values):
    out = jnp.where(steps == 3, values[3], 0.0)
    for j in (2, 1, 0):
        out = jnp.where(steps == j, values[j], out)
    return out


def spline_weights(t):
    s = 1.0 - t
    square = t * t
    cube = square * t
    return (
        s * s * s / 6.0,
        (3.0 * cube - 6.0 * square + 4.0) / 6.0,
        (-3.0 * cube + 3.0 * square + 3.0 * t + 1.0) / 6.0,
        cube / 6.0,
    )


def spline_slopes(t):
    s = 1.0 - t
    square = t * t
    return (-0.5 * s * s, 1.5 * square - 2.0 * t, -1.5 * square + t + 0.5, 0.5 * square)


def swap(value):
    return pltpu.roll(value, HALF, 1)


def exchange_lanes(blocks, lanes):
    blocks = list(blocks)
    for bit in range(3):
        step = 1 << bit
        clear = (lanes & step) == 0
        for a in range(8):
            if not a & step:
                x, y = blocks[a], blocks[a + step]
                blocks[a] = jnp.where(clear, x, pltpu.roll(y, step, 1))
                blocks[a + step] = jnp.where(clear, pltpu.roll(x, 128 - step, 1), y)
    return blocks


def far_first(sizes):
    offsets = [o for o in np.ndindex(*sizes) if any(o)]

    def hops(offset):
        return sum(min(o, size - o) for o, size in zip(offset, sizes))

    return sorted(offsets, key=lambda o: -hops(o))


def kernel(
    count_hbm,
    factor_hbm,
    offset_hbm,
    base_hbm,
    charge_hbm,
    zh_hbm,
    zl_hbm,
    yh_hbm,
    yl_hbm,
    yth_hbm,
    ytl_hbm,
    xh_hbm,
    xl_hbm,
    xth_hbm,
    xtl_hbm,
    gain_hbm,
    square_hbm,
    zfactor_hbm,
    force_ref,
    grad_ref,
    count_ref,
    factor_ref,
    offset_ref,
    base_ref,
    charge_ref,
    zh_ref,
    zl_ref,
    yh_ref,
    yl_ref,
    yth_ref,
    ytl_ref,
    xh_ref,
    xl_ref,
    xth_ref,
    xtl_ref,
    gain_ref,
    square_ref,
    zfactor_ref,
    send_a,
    recv_a,
    send_b,
    recv_b,
    send_c,
    recv_c,
    send_d,
    recv_d,
    depth_h,
    depth_l,
    slope_h,
    slope_l,
    send_sems,
    recv_sems,
    local_sems,
):
    w = lax.axis_index("wide")
    n = lax.axis_index("narrow")
    place = w // DOMAINS
    v = w % DOMAINS
    core = v % 2
    y = (v // 2) * 2 + n // 4
    x = n % 4

    def ring_mate(offset):
        other = (place + offset) % RING
        return other, (other * DOMAINS + v, n)

    def layer_mate(offset):
        dy, dx, dc = offset
        y_to = (y + dy) % 4
        v_to = (y_to // 2) * 2 + (core + dc) % 2
        n_to = (y_to % 2) * 4 + (x + dx) % 4
        return v_to, n_to, (place * DOMAINS + v_to, n_to)

    ring = [o[0] for o in far_first((RING,))]
    layer = far_first((4, 4, 2))

    barrier = pltpu.get_barrier_semaphore()
    for offset in ring:
        pl.semaphore_signal(barrier, inc=1, device_id=ring_mate(offset)[1], device_id_type=MESH)
    for offset in layer:
        pl.semaphore_signal(barrier, inc=1, device_id=layer_mate(offset)[2], device_id_type=MESH)

    inputs = (
        (count_hbm, count_ref),
        (factor_hbm, factor_ref),
        (offset_hbm, offset_ref),
        (base_hbm, base_ref),
        (charge_hbm, charge_ref),
        (zh_hbm, zh_ref),
        (zl_hbm, zl_ref),
        (yth_hbm, yth_ref),
        (ytl_hbm, ytl_ref),
        (zfactor_hbm, zfactor_ref),
        (gain_hbm, gain_ref),
        (square_hbm, square_ref),
        (xh_hbm, xh_ref),
        (xl_hbm, xl_ref),
        (xth_hbm, xth_ref),
        (xtl_hbm, xtl_ref),
        (yh_hbm, yh_ref),
        (yl_hbm, yl_ref),
    )
    loads = [pltpu.make_async_copy(a, b, local_sems.at[i]) for i, (a, b) in enumerate(inputs)]
    for load in loads:
        load.start()

    lanes = lax.broadcasted_iota(jnp.int32, (1, 128), 1)
    low_lanes = lanes < HALF
    low_rows = lax.broadcasted_iota(jnp.int32, (1, 8, 1), 1) < CX

    for load in loads[:5]:
        load.wait()
    t = [offset_ref[d, 0] for d in range(3)]
    corner = [base_ref[d, 0] for d in range(3)]
    weights = [spline_weights(u) for u in t]
    slopes = [spline_slopes(u) for u in t]
    occupied = lax.broadcasted_iota(jnp.int32, (1, SLOTS), 1) < count_ref[...]
    charge = jnp.where(occupied, charge_ref[0], 0.0)

    def depth_steps(first):
        cell = lax.broadcasted_iota(jnp.int32, (128, SLOTS), 0) + first
        return (cell - corner[2]) & (NZ - 1)

    for first in range(0, NZ, 128):
        high, low = split(pick(depth_steps(first), weights[2]))
        depth_h[first : first + 128, :] = high
        depth_l[first : first + 128, :] = low

    row_steps = lax.broadcasted_iota(jnp.int32, (16, SLOTS), 0) - corner[1]
    row_q = pick(row_steps, weights[1]) * charge
    plane_w = [pick(p - corner[0], weights[0]) for p in range(PLANES)]
    cross = jnp.concatenate([row_q * plane_w[p] for p in range(PLANES)], axis=0)
    grid = dot3(split(cross), (depth_h[...], depth_l[...]), ((1,), (1,)))
    for load in loads[5:7]:
        load.wait()
    spectrum = dot3(split(grid), (zh_ref[...], zl_ref[...]), ((1,), (0,)))
    for m in range(DOMAINS):
        tiles = [spectrum[16 * p : 16 * p + 16, 128 * m : 128 * m + 128] for p in range(PLANES)]
        tiles = exchange_lanes(tiles + [jnp.zeros((16, 128), F32)], lanes)
        for e in range(NARROW):
            send_a[16 * (8 * m + e) : 16 * (8 * m + e) + 16, :] = tiles[e]

    pl.semaphore_wait(barrier, len(ring) + len(layer))

    def push(stage, source, target, to):
        pltpu.make_async_remote_copy(
            src_ref=source,
            dst_ref=target,
            send_sem=send_sems.at[stage],
            recv_sem=recv_sems.at[stage],
            device_id=to,
            device_id_type=MESH,
        ).start()

    def drain(stage, block):
        return pltpu.make_async_remote_copy(
            src_ref=block,
            dst_ref=block,
            send_sem=send_sems.at[stage],
            recv_sem=recv_sems.at[stage],
            device_id=(w, n),
            device_id_type=MESH,
        )

    mine = 8 * v + n
    own_a = recv_a.at[pl.ds(ROWS * mine, ROWS)]
    for offset in layer:
        v_to, n_to, to = layer_mate(offset)
        push(0, send_a.at[pl.ds(16 * (8 * v_to + n_to), ROWS)], own_a, to)
    keep_a = pltpu.make_async_copy(send_a.at[pl.ds(16 * mine, ROWS)], own_a, local_sems.at[18])
    keep_a.start()

    for first in range(0, NZ, 128):
        high, low = split(pick(depth_steps(first), slopes[2]))
        slope_h[first : first + 128, :] = high
        slope_l[first : first + 128, :] = low
    for load in loads[7:]:
        load.wait()
    coefficient = 128 * v + 8 * place + n
    chosen = lax.broadcasted_iota(jnp.int32, (8, NZ), 1) == coefficient
    zfactor = jnp.sum(jnp.where(chosen, zfactor_ref[...], 0.0), axis=1, keepdims=True)
    squared = square_ref[...] + zfactor[0:1]
    positive = jnp.where(squared > 0.0, squared, 1.0)
    influence = jnp.where(squared > 0.0, gain_ref[...] * zfactor[1:2] / positive, 0.0)

    keep_a.wait()
    drain(0, recv_a.at[pl.ds(0, ROWS * 31)]).wait_recv()
    half = 8 * ROWS * 2
    rows = jnp.concatenate([recv_a[:half], recv_a[half:]], axis=1)
    columns = dot3((yth_ref[...], ytl_ref[...]), split(rows), ((1,), (0,)))
    first = columns[:, :128].T.reshape(RING, 8, 128)
    second = columns[:, 128:].T.reshape(RING, 8, 128)

    def both(value):
        return swap(value.reshape(8 * RING, 128)).reshape(RING, 8, 128)

    def turn(value):
        return pltpu.roll(value, CX, 1)

    first_swapped = both(first)
    second_swapped = both(second)
    low3 = low_lanes.reshape(1, 1, 128)
    upper = first + jnp.where(low3, 0.0, turn(first_swapped))
    lower = turn(second) + jnp.where(low3, first_swapped, second_swapped)
    send_b[:, 0:8, :] = jnp.where(low_rows, upper, lower)
    send_b[:, 8:16, :] = turn(second_swapped)

    for offset in ring:
        other, to = ring_mate(offset)
        push(1, send_b.at[other, pl.ds(0, 12)], recv_b.at[place, pl.ds(0, 12)], to)
    recv_b[place] = send_b[place]
    drain(1, recv_b.at[pl.ds(0, 15), pl.ds(0, 12)]).wait_recv()

    beyond = recv_b[:, 8:16, :]
    beyond = jnp.concatenate([beyond[RING - 1 :], beyond[: RING - 1]], axis=0)
    planes = recv_b[:, 0:8, :] + jnp.where(low_rows & low3, beyond, 0.0)
    planes = planes.reshape(8 * RING, 128)
    turned = swap(planes)
    stacked = jnp.concatenate(
        [jnp.where(low_lanes, planes, turned), jnp.where(low_lanes, turned, planes)], axis=0
    )
    filtered = dot3((xh_ref[...], xl_ref[...]), split(stacked), ((1,), (0,))) * influence
    planes = dot3((xth_ref[...], xtl_ref[...]), split(filtered), ((1,), (0,)))
    planes = jnp.where(low_lanes, planes[:128], planes[128:]).reshape(RING, 8, 128)
    send_c[:, 0:8, :] = planes
    send_c[:, 8:16, :] = jnp.concatenate([planes[1:], planes[:1]], axis=0)

    for offset in ring:
        other, to = ring_mate(offset)
        push(2, send_c.at[other, pl.ds(0, 12)], recv_c.at[place, pl.ds(0, 12)], to)
    recv_c[place] = send_c[place]
    drain(2, recv_c.at[pl.ds(0, 15), pl.ds(0, 12)]).wait_recv()

    own = recv_c[:, 0:8, :]
    own_swapped = both(own)
    beyond = turn(both(recv_c[:, 8:16, :]))
    first = jnp.where(low_rows, own, jnp.where(low3, turn(own_swapped), own_swapped))
    second = jnp.where(low_rows, turn(own), jnp.where(low3, own_swapped, beyond))
    columns = jnp.concatenate([first, second], axis=0).reshape(16 * RING, 128)
    rows = dot3((yh_ref[...], yl_ref[...]), split(columns), ((1,), (1,)))
    send_d[0] = rows[:, :128]
    send_d[1] = rows[:, 128:]

    own_d = recv_d.at[pl.ds(16 * mine, ROWS)]

    def block_d(v_to, n_to):
        return send_d.at[v_to // 2, pl.ds(ROWS * (8 * (v_to % 2) + n_to), ROWS)]

    for offset in layer:
        v_to, n_to, to = layer_mate(offset)
        push(3, block_d(v_to, n_to), own_d, to)
    keep_d = pltpu.make_async_copy(block_d(v, n), own_d, local_sems.at[19])
    keep_d.start()
    keep_d.wait()
    drain(3, recv_a.at[pl.ds(0, ROWS * 31)]).wait_recv()

    inside = lax.broadcasted_iota(jnp.int32, (16, 128), 0) < ROWS
    parts = []
    for m in range(DOMAINS):
        tiles = [recv_d[16 * (8 * m + e) : 16 * (8 * m + e) + 16, :] for e in range(NARROW)]
        tiles = exchange_lanes([jnp.where(inside, u, 0.0) for u in tiles], lanes)
        parts.append(jnp.concatenate(tiles[:PLANES], axis=0))
    spectrum = jnp.concatenate(parts, axis=1)
    potential = split(dot3(split(spectrum), (zh_ref[...], zl_ref[...]), ((1,), (1,))))
    along_w = dot3(potential, (depth_h[...], depth_l[...]), ((1,), (0,)))
    along_s = dot3(potential, (slope_h[...], slope_l[...]), ((1,), (0,)))

    total = jnp.zeros((16, SLOTS), F32)
    pull_x, pull_z = total, total
    for p in range(PLANES):
        part = slice(16 * p, 16 * p + 16)
        total = total + along_w[part] * plane_w[p]
        pull_x = pull_x + along_w[part] * pick(p - corner[0], slopes[0])
        pull_z = pull_z + along_s[part] * plane_w[p]

    def over_rows(value):
        return jnp.sum(value, axis=0, keepdims=True)

    factor = factor_ref[...]
    row_w = pick(row_steps, weights[1])
    pull_y = over_rows(total * pick(row_steps, slopes[1]))
    total = over_rows(total * row_w)
    pull_x = over_rows(pull_x * row_w)
    pull_z = over_rows(pull_z * row_w)
    grad_ref[0] = jnp.where(occupied, factor * total, 0.0)
    pull = -factor * charge
    force_ref[0, 0] = pull * pull_x
    force_ref[1, 0] = pull * pull_y
    force_ref[2, 0] = pull * pull_z

    drain(0, recv_a.at[pl.ds(0, ROWS * 31)]).wait_send()
    drain(1, recv_b.at[pl.ds(0, 15), pl.ds(0, 12)]).wait_send()
    drain(2, recv_c.at[pl.ds(0, 15), pl.ds(0, 12)]).wait_send()
    drain(3, recv_a.at[pl.ds(0, ROWS * 31)]).wait_send()


def on_device(offsets, bases, charges, counts, cotangent):
    z_pair = halves(real_basis(NZ)[0].T)
    y_table = row_matrix()
    x_table = real_basis(NX)[0][:, plane_order()]
    square_x, gain_x = frequency_factors(NX)
    square_y, gain_y = frequency_factors(NY)
    zfactor = np.zeros((8, NZ), np.float32)
    zfactor[0], zfactor[1] = frequency_factors(NZ)
    square = (square_x[:, None] + np.tile(square_y, 2)[None, :]).astype(np.float32)
    gain = (gain_x[:, None] * np.tile(gain_y, 2)[None, :] / math.pi).astype(np.float32)
    arrays = (
        counts,
        cotangent,
        offsets,
        bases,
        charges,
        *z_pair,
        *halves(y_table),
        *halves(y_table.T),
        *halves(x_table),
        *halves(x_table.T),
        gain,
        square,
        zfactor,
    )
    hbm = pl.BlockSpec(memory_space=pltpu.HBM)
    vmem = pl.BlockSpec(memory_space=VMEM)
    return pl.pallas_call(
        kernel,
        out_shape=(
            jax.ShapeDtypeStruct((3, 1, 1, SLOTS), F32),
            jax.ShapeDtypeStruct((1, 1, SLOTS), F32),
        ),
        in_specs=[hbm] * len(arrays),
        out_specs=(vmem, vmem),
        scratch_shapes=[
            *[VMEM(a.shape, a.dtype) for a in arrays],
            VMEM((16 * 32, 128), F32),
            VMEM((ROWS * 32, 128), F32),
            VMEM((RING, 16, 128), F32),
            VMEM((RING, 16, 128), F32),
            VMEM((RING, 16, 128), F32),
            VMEM((RING, 16, 128), F32),
            VMEM((2, ROWS * 16, 128), F32),
            VMEM((16 * 32, 128), F32),
            VMEM((NZ, SLOTS), BF16),
            VMEM((NZ, SLOTS), BF16),
            VMEM((NZ, SLOTS), BF16),
            VMEM((NZ, SLOTS), BF16),
            pltpu.SemaphoreType.DMA((4,)),
            pltpu.SemaphoreType.DMA((4,)),
            pltpu.SemaphoreType.DMA((len(arrays) + 2,)),
        ],
        compiler_params=pltpu.CompilerParams(
            collective_id=0, has_side_effects=True, vmem_limit_bytes=63 * 1024 * 1024
        ),
        name="ewald",
    )(*arrays)


def solution(mesh):
    placed = (
        P(None, "wide", "narrow", None),
        P(None, "wide", "narrow", None),
        P("wide", "narrow", None),
        P("wide", "narrow"),
        P(),
    )
    return jax.shard_map(
        on_device,
        mesh=mesh,
        in_specs=placed,
        out_specs=(P(None, "wide", "narrow", None), P("wide", "narrow", None)),
        check_vma=False,
    )
```

time: 70.1 us -> 49.4 us (0.70)
  local copies, waits for them, and re-layouts: 13.4 us -> 1.87 us
  Pallas kernels: 54.2 us -> 45.4 us
    unnamed x36 -> x4, local copies, waits for them, and re-layouts: 13.4 us -> 1.87 us
    pallas_call x1, Pallas kernels: 54.2 us -> 45.4 us  [on_device(): pl.pallas_call(kernel, out_shape=(jax.ShapeDtypeStruct((3, 1, 1, SLOTS),...]
where the time goes in v2:
time: 49.4 us; the launch traced here: 49.2 us
  Pallas kernels  45.4 us (92%)
  between operations  1.94 us (4%)
  local copies, waits for them, and re-layouts  1.87 us (4%)
    pallas_call x1, Pallas kernels, on_device(): pl.pallas_call(kernel, out_shape=(jax.ShapeDtypeStruct((3, 1, 1, SLOTS),...  45.4 us
    unnamed x4, local copies, waits for them, and re-layouts  1.87 us

profile of v2, /device:TPU:1, one launch (start us, length us, event | category | flops | bytes accessed | tf_op | source)
XLA Modules:
  0.0 49.2 jit_solution(8203604835855745842)
XLA Ops:
  1.9 45.4 %ewald.1 = (f32[3,1,1,512]{3,2,1,0:T(1,128)}, f32[1,1,512]{2,1,0:T(1,128)}) custom-call(s32[1,1]{1,0:T(1,128)S(6)} %copy.22.count_hbm, f32[1]{0:T(128)S(6)} %copy.23.factor_hbm, f32[3,1,1,512]{3,2,1,0:T(1,128)} %offset_hbm.1, s32[3,1,1,512]{3,2,1,0:T(1,128)} %base_hbm.1, f32[1,1,512]{2,1,0:T(1,128)} %charge_hbm.1, bf16[512,512]{1,0:T(8,128)(2,1)} %constant.26.clone.zh_hbm, ...), custom_call_target="tpu_custom_call" | custom-call | tf_op jit(solution)/shard_map/ewald/pallas_call | solution.py:460
  47.3 0.0 copy-start
  47.3 1.3 %copy.24 = f32[3,1,1,512]{3,2,1,0:T(1,128)} copy(f32[3,1,1,512]{3,2,1,0:T(1,128)} %get-tuple-element.4) | data formatting | bytes 12288
  48.6 0.0 copy-done
  48.6 0.6 %copy.25 = f32[1,1,512]{2,1,0:T(1,128)} copy(f32[1,1,512]{2,1,0:T(1,128)S(1)} %copy-done) | data formatting | bytes 4096
Async XLA Ops:
  47.3 1.3 %copy-start = (f32[1,1,512]{2,1,0:T(1,128)S(1)}, f32[1,1,512]{2,1,0:T(1,128)}, u32[]{:S(2)}) copy-start(f32[1,1,512]{2,1,0:T(1,128)} %get-tuple-element.5) | copy-start | bytes 6148

commit v3 on v2

--- a/solution.py
+++ b/solution.py
@@ -21,6 +21,7 @@
 RING = 16
 DOMAINS = WIDE // RING
 PLANES = CX + 3
+REACH = RING // 4
 HALF = 64
 MESH = pl.DeviceIdType.MESH
 VMEM = pltpu.VMEM
@@ -141,6 +142,8 @@
     charge_hbm,
     zh_hbm,
     zl_hbm,
+    zth_hbm,
+    ztl_hbm,
     yh_hbm,
     yl_hbm,
     yth_hbm,
@@ -152,8 +155,7 @@
     gain_hbm,
     square_hbm,
     zfactor_hbm,
-    force_ref,
-    grad_ref,
+    raw_ref,
     count_ref,
     factor_ref,
     offset_ref,
@@ -161,6 +163,8 @@
     charge_ref,
     zh_ref,
     zl_ref,
+    zth_ref,
+    ztl_ref,
     yh_ref,
     yl_ref,
     yth_ref,
@@ -182,11 +186,12 @@
     recv_d,
     depth_h,
     depth_l,
-    slope_h,
-    slope_l,
+    atom_h,
+    atom_l,
     send_sems,
     recv_sems,
     local_sems,
+    ring_sem,
 ):
     w = lax.axis_index("wide")
     n = lax.axis_index("narrow")
@@ -211,7 +216,8 @@
     layer = far_first((4, 4, 2))
 
     barrier = pltpu.get_barrier_semaphore()
-    for offset in ring:
+    near = [o for o in ring if min(o, RING - o) <= REACH]
+    for offset in near:
         pl.semaphore_signal(barrier, inc=1, device_id=ring_mate(offset)[1], device_id_type=MESH)
     for offset in layer:
         pl.semaphore_signal(barrier, inc=1, device_id=layer_mate(offset)[2], device_id_type=MESH)
@@ -235,6 +241,8 @@
         (xtl_hbm, xtl_ref),
         (yh_hbm, yh_ref),
         (yl_hbm, yl_ref),
+        (zth_hbm, zth_ref),
+        (ztl_hbm, ztl_ref),
     )
     loads = [pltpu.make_async_copy(a, b, local_sems.at[i]) for i, (a, b) in enumerate(inputs)]
     for load in loads:
@@ -259,14 +267,15 @@
 
     for first in range(0, NZ, 128):
         high, low = split(pick(depth_steps(first), weights[2]))
-        depth_h[first : first + 128, :] = high
-        depth_l[first : first + 128, :] = low
+        depth_h[first : first + 128, :SLOTS] = high
+        depth_l[first : first + 128, :SLOTS] = low
 
     row_steps = lax.broadcasted_iota(jnp.int32, (16, SLOTS), 0) - corner[1]
-    row_q = pick(row_steps, weights[1]) * charge
+    row_w = pick(row_steps, weights[1])
+    row_q = row_w * charge
     plane_w = [pick(p - corner[0], weights[0]) for p in range(PLANES)]
     cross = jnp.concatenate([row_q * plane_w[p] for p in range(PLANES)], axis=0)
-    grid = dot3(split(cross), (depth_h[...], depth_l[...]), ((1,), (1,)))
+    grid = dot3(split(cross), (depth_h[:, :SLOTS], depth_l[:, :SLOTS]), ((1,), (1,)))
     for load in loads[5:7]:
         load.wait()
     spectrum = dot3(split(grid), (zh_ref[...], zl_ref[...]), ((1,), (0,)))
@@ -276,7 +285,7 @@
         for e in range(NARROW):
             send_a[16 * (8 * m + e) : 16 * (8 * m + e) + 16, :] = tiles[e]
 
-    pl.semaphore_wait(barrier, len(ring) + len(layer))
+    pl.semaphore_wait(barrier, len(near) + len(layer))
 
     def push(stage, source, target, to):
         pltpu.make_async_remote_copy(
@@ -303,13 +312,17 @@
     for offset in layer:
         v_to, n_to, to = layer_mate(offset)
         push(0, send_a.at[pl.ds(16 * (8 * v_to + n_to), ROWS)], own_a, to)
-    keep_a = pltpu.make_async_copy(send_a.at[pl.ds(16 * mine, ROWS)], own_a, local_sems.at[18])
+    keep_a = pltpu.make_async_copy(send_a.at[pl.ds(16 * mine, ROWS)], own_a, local_sems.at[20])
     keep_a.start()
-
+    for offset in (REACH, RING - REACH):
+        pl.semaphore_signal(ring_sem, inc=1, device_id=ring_mate(offset)[1], device_id_type=MESH)
+
+    row_s = pick(row_steps, slopes[1])
+    plane_s = [pick(p - corner[0], slopes[0]) for p in range(PLANES)]
     for first in range(0, NZ, 128):
         high, low = split(pick(depth_steps(first), slopes[2]))
-        slope_h[first : first + 128, :] = high
-        slope_l[first : first + 128, :] = low
+        depth_h[first : first + 128, SLOTS:] = high
+        depth_l[first : first + 128, SLOTS:] = low
     for load in loads[7:]:
         load.wait()
     coefficient = 128 * v + 8 * place + n
@@ -341,10 +354,17 @@
     send_b[:, 0:8, :] = jnp.where(low_rows, upper, lower)
     send_b[:, 8:16, :] = turn(second_swapped)
 
+    pl.semaphore_wait(ring_sem, 2)
     for offset in ring:
         other, to = ring_mate(offset)
         push(1, send_b.at[other, pl.ds(0, 12)], recv_b.at[place, pl.ds(0, 12)], to)
     recv_b[place] = send_b[place]
+    for first in range(0, NZ, 128):
+        part = slice(first, first + 128)
+        z_rows = (zth_ref[part, :], ztl_ref[part, :])
+        high, low = split(dot3(z_rows, (depth_h[...], depth_l[...]), ((1,), (0,))))
+        atom_h[part, :] = high
+        atom_l[part, :] = low
     drain(1, recv_b.at[pl.ds(0, 15), pl.ds(0, 12)]).wait_recv()
 
     beyond = recv_b[:, 8:16, :]
@@ -385,7 +405,7 @@
     for offset in layer:
         v_to, n_to, to = layer_mate(offset)
         push(3, block_d(v_to, n_to), own_d, to)
-    keep_d = pltpu.make_async_copy(block_d(v, n), own_d, local_sems.at[19])
+    keep_d = pltpu.make_async_copy(block_d(v, n), own_d, local_sems.at[21])
     keep_d.start()
     keep_d.wait()
     drain(3, recv_a.at[pl.ds(0, ROWS * 31)]).wait_recv()
@@ -397,32 +417,29 @@
         tiles = exchange_lanes([jnp.where(inside, u, 0.0) for u in tiles], lanes)
         parts.append(jnp.concatenate(tiles[:PLANES], axis=0))
     spectrum = jnp.concatenate(parts, axis=1)
-    potential = split(dot3(split(spectrum), (zh_ref[...], zl_ref[...]), ((1,), (1,))))
-    along_w = dot3(potential, (depth_h[...], depth_l[...]), ((1,), (0,)))
-    along_s = dot3(potential, (slope_h[...], slope_l[...]), ((1,), (0,)))
+    along = dot3(split(spectrum), (atom_h[...], atom_l[...]), ((1,), (0,)))
 
     total = jnp.zeros((16, SLOTS), F32)
     pull_x, pull_z = total, total
     for p in range(PLANES):
         part = slice(16 * p, 16 * p + 16)
-        total = total + along_w[part] * plane_w[p]
-        pull_x = pull_x + along_w[part] * pick(p - corner[0], slopes[0])
-        pull_z = pull_z + along_s[part] * plane_w[p]
+        total = total + along[part, :SLOTS] * plane_w[p]
+        pull_x = pull_x + along[part, :SLOTS] * plane_s[p]
+        pull_z = pull_z + along[part, SLOTS:] * plane_w[p]
 
     def over_rows(value):
         return jnp.sum(value, axis=0, keepdims=True)
 
     factor = factor_ref[...]
-    row_w = pick(row_steps, weights[1])
-    pull_y = over_rows(total * pick(row_steps, slopes[1]))
+    pull_y = over_rows(total * row_s)
     total = over_rows(total * row_w)
     pull_x = over_rows(pull_x * row_w)
     pull_z = over_rows(pull_z * row_w)
-    grad_ref[0] = jnp.where(occupied, factor * total, 0.0)
     pull = -factor * charge
-    force_ref[0, 0] = pull * pull_x
-    force_ref[1, 0] = pull * pull_y
-    force_ref[2, 0] = pull * pull_z
+    raw_ref[0, 0] = pull * pull_x
+    raw_ref[1, 0] = pull * pull_y
+    raw_ref[2, 0] = pull * pull_z
+    raw_ref[3, 0] = jnp.where(occupied, factor * total, 0.0)
 
     drain(0, recv_a.at[pl.ds(0, ROWS * 31)]).wait_send()
     drain(1, recv_b.at[pl.ds(0, 15), pl.ds(0, 12)]).wait_send()
@@ -430,8 +447,13 @@
     drain(3, recv_a.at[pl.ds(0, ROWS * 31)]).wait_send()
 
 
+def hand_out(raw_ref, force_ref, grad_ref):
+    force_ref[...] = raw_ref[0:3]
+    grad_ref[...] = raw_ref[3]
+
+
 def on_device(offsets, bases, charges, counts, cotangent):
-    z_pair = halves(real_basis(NZ)[0].T)
+    z_table = real_basis(NZ)[0].T
     y_table = row_matrix()
     x_table = real_basis(NX)[0][:, plane_order()]
     square_x, gain_x = frequency_factors(NX)
@@ -446,7 +468,8 @@
         offsets,
         bases,
         charges,
-        *z_pair,
+        *halves(z_table),
+        *halves(z_table.T),
         *halves(y_table),
         *halves(y_table.T),
         *halves(x_table),
@@ -457,14 +480,11 @@
     )
     hbm = pl.BlockSpec(memory_space=pltpu.HBM)
     vmem = pl.BlockSpec(memory_space=VMEM)
-    return pl.pallas_call(
+    raw = pl.pallas_call(
         kernel,
-        out_shape=(
-            jax.ShapeDtypeStruct((3, 1, 1, SLOTS), F32),
-            jax.ShapeDtypeStruct((1, 1, SLOTS), F32),
-        ),
+        out_shape=jax.ShapeDtypeStruct((4, 1, 1, SLOTS), F32),
         in_specs=[hbm] * len(arrays),
-        out_specs=(vmem, vmem),
+        out_specs=vmem,
         scratch_shapes=[
             *[VMEM(a.shape, a.dtype) for a in arrays],
             VMEM((16 * 32, 128), F32),
@@ -475,19 +495,30 @@
             VMEM((RING, 16, 128), F32),
             VMEM((2, ROWS * 16, 128), F32),
             VMEM((16 * 32, 128), F32),
-            VMEM((NZ, SLOTS), BF16),
-            VMEM((NZ, SLOTS), BF16),
-            VMEM((NZ, SLOTS), BF16),
-            VMEM((NZ, SLOTS), BF16),
+            VMEM((NZ, 2 * SLOTS), BF16),
+            VMEM((NZ, 2 * SLOTS), BF16),
+            VMEM((NZ, 2 * SLOTS), BF16),
+            VMEM((NZ, 2 * SLOTS), BF16),
             pltpu.SemaphoreType.DMA((4,)),
             pltpu.SemaphoreType.DMA((4,)),
             pltpu.SemaphoreType.DMA((len(arrays) + 2,)),
+            pltpu.SemaphoreType.REGULAR,
         ],
         compiler_params=pltpu.CompilerParams(
             collective_id=0, has_side_effects=True, vmem_limit_bytes=63 * 1024 * 1024
         ),
         name="ewald",
     )(*arrays)
+    return pl.pallas_call(
+        hand_out,
+        out_shape=(
+            jax.ShapeDtypeStruct((3, 1, 1, SLOTS), F32),
+            jax.ShapeDtypeStruct((1, 1, SLOTS), F32),
+        ),
+        in_specs=[vmem],
+        out_specs=(vmem, vmem),
+        name="hand_out",
+    )(raw)
 
 
 def solution(mesh):

time: 49.4 us -> 46.6 us (0.943)
  local copies, waits for them, and re-layouts: 1.87 us -> 0 us
  Pallas kernels: 45.4 us -> 44.5 us
    unnamed x4 -> x0, local copies, waits for them, and re-layouts: 1.87 us -> none
    pallas_call x1 -> x2, Pallas kernels: 45.4 us -> 44.5 us  [the longest x1 43.2 us: on_device(): pl.pallas_call(kernel, out_shape=jax.ShapeDtypeStruct((4, 1, 1, SLOTS), F...]
where the time goes in v3:
time: 46.6 us; the launch traced here: 46.4 us
  Pallas kernels  44.5 us (95%)
  between operations  1.93 us (4%)
    pallas_call x1, Pallas kernels, on_device(): pl.pallas_call(kernel, out_shape=jax.ShapeDtypeStruct((4, 1, 1, SLOTS), F...  43.2 us
    pallas_call x1, Pallas kernels, on_device(): pl.pallas_call(hand_out, out_shape=(jax.ShapeDtypeStruct((3, 1, 1, SLOTS)...  1.3 us

profile of v3, /device:TPU:1, one launch (start us, length us, event | category | flops | bytes accessed | tf_op | source)
XLA Modules:
  0.0 46.4 jit_solution(9097543352376020682)
XLA Ops:
  1.9 43.2 %ewald.1.raw_ref = f32[4,1,1,512]{3,2,1,0:T(1,128)} custom-call(s32[1,1]{1,0:T(1,128)S(6)} %copy.22.count_hbm, f32[1]{0:T(128)S(6)} %copy.23.factor_hbm, f32[3,1,1,512]{3,2,1,0:T(1,128)} %offset_hbm.1, s32[3,1,1,512]{3,2,1,0:T(1,128)} %base_hbm.1, f32[1,1,512]{2,1,0:T(1,128)} %charge_hbm.1, bf16[512,512]{1,0:T(8,128)(2,1)} %constant.30.clone.zh_hbm, ...), custom_call_target="tpu_custom_call" | custom-call | tf_op jit(solution)/shard_map/ewald/pallas_call | solution.py:483
  45.1 1.3 %hand_out.1 = (f32[3,1,1,512]{3,2,1,0:T(1,128)}, f32[1,1,512]{2,1,0:T(1,128)}) custom-call(f32[4,1,1,512]{3,2,1,0:T(1,128)} %ewald.1.raw_ref), custom_call_target="tpu_custom_call" | custom-call | tf_op jit(solution)/shard_map/hand_out/pallas_call | solution.py:512

commit v4 on v3

--- a/solution.py
+++ b/solution.py
@@ -135,8 +135,8 @@
 
 
 def kernel(
-    count_hbm,
-    factor_hbm,
+    count_ref,
+    factor_ref,
     offset_hbm,
     base_hbm,
     charge_hbm,
@@ -156,8 +156,6 @@
     square_hbm,
     zfactor_hbm,
     raw_ref,
-    count_ref,
-    factor_ref,
     offset_ref,
     base_ref,
     charge_ref,
@@ -195,36 +193,31 @@
 ):
     w = lax.axis_index("wide")
     n = lax.axis_index("narrow")
-    place = w // DOMAINS
-    v = w % DOMAINS
-    core = v % 2
-    y = (v // 2) * 2 + n // 4
-    x = n % 4
+    place = lax.div(w, DOMAINS)
+    v = lax.rem(w, DOMAINS)
+    core = lax.rem(v, 2)
+    y = lax.div(v, 2) * 2 + lax.div(n, 4)
+    x = lax.rem(n, 4)
+    ys = [lax.rem(y + i, 4) for i in range(4)]
+    xs = [lax.rem(x + i, 4) for i in range(4)]
+    cores = [core, 1 - core]
+    vs = [[lax.div(j, 2) * 2 + c for c in cores] for j in ys]
+    ns = [[lax.rem(j, 2) * 4 + i for i in xs] for j in ys]
 
     def ring_mate(offset):
-        other = (place + offset) % RING
+        other = lax.rem(place + offset, RING)
         return other, (other * DOMAINS + v, n)
 
     def layer_mate(offset):
         dy, dx, dc = offset
-        y_to = (y + dy) % 4
-        v_to = (y_to // 2) * 2 + (core + dc) % 2
-        n_to = (y_to % 2) * 4 + (x + dx) % 4
+        v_to, n_to = vs[dy][dc], ns[dy][dx]
         return v_to, n_to, (place * DOMAINS + v_to, n_to)
 
     ring = [o[0] for o in far_first((RING,))]
     layer = far_first((4, 4, 2))
 
     barrier = pltpu.get_barrier_semaphore()
-    near = [o for o in ring if min(o, RING - o) <= REACH]
-    for offset in near:
-        pl.semaphore_signal(barrier, inc=1, device_id=ring_mate(offset)[1], device_id_type=MESH)
-    for offset in layer:
-        pl.semaphore_signal(barrier, inc=1, device_id=layer_mate(offset)[2], device_id_type=MESH)
-
     inputs = (
-        (count_hbm, count_ref),
-        (factor_hbm, factor_ref),
         (offset_hbm, offset_ref),
         (base_hbm, base_ref),
         (charge_hbm, charge_ref),
@@ -245,20 +238,30 @@
         (ztl_hbm, ztl_ref),
     )
     loads = [pltpu.make_async_copy(a, b, local_sems.at[i]) for i, (a, b) in enumerate(inputs)]
-    for load in loads:
+    for load in loads[:3]:
+        load.start()
+
+    near = [o for o in ring if min(o, RING - o) <= REACH]
+    mates = [ring_mate(offset)[1] for offset in near[:2]]
+    mates += [layer_mate(offset)[2] for offset in layer]
+    mates += [ring_mate(offset)[1] for offset in near[2:]]
+    for mate in mates:
+        pl.semaphore_signal(barrier, inc=1, device_id=mate, device_id_type=MESH)
+
+    for load in loads[3:]:
         load.start()
 
     lanes = lax.broadcasted_iota(jnp.int32, (1, 128), 1)
     low_lanes = lanes < HALF
     low_rows = lax.broadcasted_iota(jnp.int32, (1, 8, 1), 1) < CX
 
-    for load in loads[:5]:
+    for load in loads[:3]:
         load.wait()
     t = [offset_ref[d, 0] for d in range(3)]
     corner = [base_ref[d, 0] for d in range(3)]
     weights = [spline_weights(u) for u in t]
     slopes = [spline_slopes(u) for u in t]
-    occupied = lax.broadcasted_iota(jnp.int32, (1, SLOTS), 1) < count_ref[...]
+    occupied = lax.broadcasted_iota(jnp.int32, (1, SLOTS), 1) < count_ref[0, 0]
     charge = jnp.where(occupied, charge_ref[0], 0.0)
 
     def depth_steps(first):
@@ -276,7 +279,7 @@
     plane_w = [pick(p - corner[0], weights[0]) for p in range(PLANES)]
     cross = jnp.concatenate([row_q * plane_w[p] for p in range(PLANES)], axis=0)
     grid = dot3(split(cross), (depth_h[:, :SLOTS], depth_l[:, :SLOTS]), ((1,), (1,)))
-    for load in loads[5:7]:
+    for load in loads[3:5]:
         load.wait()
     spectrum = dot3(split(grid), (zh_ref[...], zl_ref[...]), ((1,), (0,)))
     for m in range(DOMAINS):
@@ -312,7 +315,7 @@
     for offset in layer:
         v_to, n_to, to = layer_mate(offset)
         push(0, send_a.at[pl.ds(16 * (8 * v_to + n_to), ROWS)], own_a, to)
-    keep_a = pltpu.make_async_copy(send_a.at[pl.ds(16 * mine, ROWS)], own_a, local_sems.at[20])
+    keep_a = pltpu.make_async_copy(send_a.at[pl.ds(16 * mine, ROWS)], own_a, local_sems.at[18])
     keep_a.start()
     for offset in (REACH, RING - REACH):
         pl.semaphore_signal(ring_sem, inc=1, device_id=ring_mate(offset)[1], device_id_type=MESH)
@@ -323,7 +326,7 @@
         high, low = split(pick(depth_steps(first), slopes[2]))
         depth_h[first : first + 128, SLOTS:] = high
         depth_l[first : first + 128, SLOTS:] = low
-    for load in loads[7:]:
+    for load in loads[5:]:
         load.wait()
     coefficient = 128 * v + 8 * place + n
     chosen = lax.broadcasted_iota(jnp.int32, (8, NZ), 1) == coefficient
@@ -400,12 +403,12 @@
     own_d = recv_d.at[pl.ds(16 * mine, ROWS)]
 
     def block_d(v_to, n_to):
-        return send_d.at[v_to // 2, pl.ds(ROWS * (8 * (v_to % 2) + n_to), ROWS)]
+        return send_d.at[lax.div(v_to, 2), pl.ds(ROWS * (8 * lax.rem(v_to, 2) + n_to), ROWS)]
 
     for offset in layer:
         v_to, n_to, to = layer_mate(offset)
         push(3, block_d(v_to, n_to), own_d, to)
-    keep_d = pltpu.make_async_copy(block_d(v, n), own_d, local_sems.at[21])
+    keep_d = pltpu.make_async_copy(block_d(v, n), own_d, local_sems.at[19])
     keep_d.start()
     keep_d.wait()
     drain(3, recv_a.at[pl.ds(0, ROWS * 31)]).wait_recv()
@@ -430,7 +433,7 @@
     def over_rows(value):
         return jnp.sum(value, axis=0, keepdims=True)
 
-    factor = factor_ref[...]
+    factor = factor_ref[0]
     pull_y = over_rows(total * row_s)
     total = over_rows(total * row_w)
     pull_x = over_rows(pull_x * row_w)
@@ -463,8 +466,6 @@
     square = (square_x[:, None] + np.tile(square_y, 2)[None, :]).astype(np.float32)
     gain = (gain_x[:, None] * np.tile(gain_y, 2)[None, :] / math.pi).astype(np.float32)
     arrays = (
-        counts,
-        cotangent,
         offsets,
         bases,
         charges,
@@ -478,12 +479,13 @@
         square,
         zfactor,
     )
+    smem = pl.BlockSpec(memory_space=pltpu.SMEM)
     hbm = pl.BlockSpec(memory_space=pltpu.HBM)
     vmem = pl.BlockSpec(memory_space=VMEM)
     raw = pl.pallas_call(
         kernel,
         out_shape=jax.ShapeDtypeStruct((4, 1, 1, SLOTS), F32),
-        in_specs=[hbm] * len(arrays),
+        in_specs=[smem] * 2 + [hbm] * len(arrays),
         out_specs=vmem,
         scratch_shapes=[
             *[VMEM(a.shape, a.dtype) for a in arrays],
@@ -505,10 +507,10 @@
             pltpu.SemaphoreType.REGULAR,
         ],
         compiler_params=pltpu.CompilerParams(
-            collective_id=0, has_side_effects=True, vmem_limit_bytes=63 * 1024 * 1024
+            collective_id=0, has_side_effects=True, vmem_limit_bytes=40 * 1024 * 1024
         ),
         name="ewald",
-    )(*arrays)
+    )(counts, cotangent, *[pltpu.with_memory_space_constraint(a, pltpu.HBM) for a in arrays])
     return pl.pallas_call(
         hand_out,
         out_shape=(
@@ -518,7 +520,7 @@
         in_specs=[vmem],
         out_specs=(vmem, vmem),
         name="hand_out",
-    )(raw)
+    )(pltpu.with_memory_space_constraint(raw, VMEM))
 
 
 def solution(mesh):

time: 46.6 us -> 45.4 us (0.974)
  Pallas kernels: 44.5 us -> 43.3 us
    pallas_call x1, Pallas kernels: 1.3 us -> 0.6 us  [on_device(): pl.pallas_call(hand_out, out_shape=(jax.ShapeDtypeStruct((3, 1, 1, SLOTS)...]
    pallas_call x1, Pallas kernels: 43.2 us -> 42.7 us  [on_device(): pl.pallas_call(kernel, out_shape=jax.ShapeDtypeStruct((4, 1, 1, SLOTS), F...]
where the time goes in v4:
time: 45.4 us; the launch traced here: 45.2 us
  Pallas kernels  43.3 us (95%)
  between operations  1.93 us (4%)
    pallas_call x1, Pallas kernels, on_device(): pl.pallas_call(kernel, out_shape=jax.ShapeDtypeStruct((4, 1, 1, SLOTS), F...  42.7 us

profile of v4, /device:TPU:1, one launch (start us, length us, event | category | flops | bytes accessed | tf_op | source)
XLA Modules:
  0.0 45.2 jit_solution(15056671714509104155)
XLA Ops:
  1.9 42.7 %ewald.1.raw_ref = f32[4,1,1,512]{3,2,1,0:T(1,128)S(1)} custom-call(s32[1,1]{1,0:T(1,128)S(6)} %copy.22.count_ref, f32[1]{0:T(128)S(6)} %copy.23.factor_ref, f32[3,1,1,512]{3,2,1,0:T(1,128)} %offset_hbm.1, s32[3,1,1,512]{3,2,1,0:T(1,128)} %base_hbm.1, f32[1,1,512]{2,1,0:T(1,128)} %charge_hbm.1, bf16[512,512]{1,0:T(8,128)(2,1)} %constant.30.clone.zh_hbm, ...), custom_call_target="tpu_custom_call" | custom-call | tf_op jit(solution)/shard_map/ewald/pallas_call | solution.py:485
  44.6 0.6 %hand_out.1 = (f32[3,1,1,512]{3,2,1,0:T(1,128)}, f32[1,1,512]{2,1,0:T(1,128)}) custom-call(f32[4,1,1,512]{3,2,1,0:T(1,128)S(1)} %ewald.1.raw_ref), custom_call_target="tpu_custom_call" | custom-call | tf_op jit(solution)/shard_map/hand_out/pallas_call | solution.py:514

commit v5 on v4

--- a/solution.py
+++ b/solution.py
@@ -76,11 +76,21 @@
 
 def dot3(a, b, contract):
     dims = (contract, ((), ()))
-
-    def one(x, y):
-        return lax.dot_general(x, y, dims, preferred_element_type=F32)
-
-    return one(a[0], b[0]) + (one(a[0], b[1]) + one(a[1], b[0]))
+    both = lax.dot_general(
+        jnp.concatenate(a, axis=0), b[0], dims, preferred_element_type=F32
+    )
+    rows = a[0].shape[0]
+    return (both[:rows] + both[rows:]) + lax.dot_general(
+        a[0], b[1], dims, preferred_element_type=F32
+    )
+
+
+def dot3_wide(a, b):
+    columns = b[0].shape[1]
+    both = jnp.dot(a[0], jnp.concatenate(b, axis=1), preferred_element_type=F32)
+    return (both[:, :columns] + both[:, columns:]) + jnp.dot(
+        a[1], b[0], preferred_element_type=F32
+    )
 
 
 def pick(steps, values):
@@ -186,6 +196,7 @@
     depth_l,
     atom_h,
     atom_l,
+    along_ref,
     send_sems,
     recv_sems,
     local_sems,
@@ -290,12 +301,12 @@
 
     pl.semaphore_wait(barrier, len(near) + len(layer))
 
-    def push(stage, source, target, to):
+    def push(stage, source, target, to, far=0):
         pltpu.make_async_remote_copy(
             src_ref=source,
             dst_ref=target,
             send_sem=send_sems.at[stage],
-            recv_sem=recv_sems.at[stage],
+            recv_sem=recv_sems.at[stage + far],
             device_id=to,
             device_id_type=MESH,
         ).start()
@@ -310,6 +321,9 @@
             device_id_type=MESH,
         )
 
+    for offset in (REACH, RING - REACH):
+        pl.semaphore_signal(ring_sem, inc=1, device_id=ring_mate(offset)[1], device_id_type=MESH)
+
     mine = 8 * v + n
     own_a = recv_a.at[pl.ds(ROWS * mine, ROWS)]
     for offset in layer:
@@ -317,8 +331,6 @@
         push(0, send_a.at[pl.ds(16 * (8 * v_to + n_to), ROWS)], own_a, to)
     keep_a = pltpu.make_async_copy(send_a.at[pl.ds(16 * mine, ROWS)], own_a, local_sems.at[18])
     keep_a.start()
-    for offset in (REACH, RING - REACH):
-        pl.semaphore_signal(ring_sem, inc=1, device_id=ring_mate(offset)[1], device_id_type=MESH)
 
     row_s = pick(row_steps, slopes[1])
     plane_s = [pick(p - corner[0], slopes[0]) for p in range(PLANES)]
@@ -378,8 +390,8 @@
     stacked = jnp.concatenate(
         [jnp.where(low_lanes, planes, turned), jnp.where(low_lanes, turned, planes)], axis=0
     )
-    filtered = dot3((xh_ref[...], xl_ref[...]), split(stacked), ((1,), (0,))) * influence
-    planes = dot3((xth_ref[...], xtl_ref[...]), split(filtered), ((1,), (0,)))
+    filtered = dot3_wide((xh_ref[...], xl_ref[...]), split(stacked)) * influence
+    planes = dot3_wide((xth_ref[...], xtl_ref[...]), split(filtered))
     planes = jnp.where(low_lanes, planes[:128], planes[128:]).reshape(RING, 8, 128)
     send_c[:, 0:8, :] = planes
     send_c[:, 8:16, :] = jnp.concatenate([planes[1:], planes[:1]], axis=0)
@@ -407,20 +419,30 @@
 
     for offset in layer:
         v_to, n_to, to = layer_mate(offset)
-        push(3, block_d(v_to, n_to), own_d, to)
+        far = lax.rem(lax.div(v_to, 2) + lax.div(v, 2), 2)
+        push(3, block_d(v_to, n_to), own_d, to, far)
     keep_d = pltpu.make_async_copy(block_d(v, n), own_d, local_sems.at[19])
     keep_d.start()
+
+    inside = lax.broadcasted_iota(jnp.int32, (16, 128), 0) < ROWS
+
+    def along_half(which):
+        parts = []
+        for m in range(2):
+            start = 256 * which + 128 * m
+            tiles = [recv_d[pl.ds(start + 16 * e, 16), :] for e in range(NARROW)]
+            tiles = exchange_lanes([jnp.where(inside, u, 0.0) for u in tiles], lanes)
+            parts.append(jnp.concatenate(tiles[:PLANES], axis=0))
+        spectrum = split(jnp.concatenate(parts, axis=1))
+        start = pl.multiple_of(256 * which, 256)
+        atoms = (atom_h[pl.ds(start, 256), :], atom_l[pl.ds(start, 256), :])
+        return dot3(spectrum, atoms, ((1,), (0,)))
+
     keep_d.wait()
-    drain(3, recv_a.at[pl.ds(0, ROWS * 31)]).wait_recv()
-
-    inside = lax.broadcasted_iota(jnp.int32, (16, 128), 0) < ROWS
-    parts = []
-    for m in range(DOMAINS):
-        tiles = [recv_d[16 * (8 * m + e) : 16 * (8 * m + e) + 16, :] for e in range(NARROW)]
-        tiles = exchange_lanes([jnp.where(inside, u, 0.0) for u in tiles], lanes)
-        parts.append(jnp.concatenate(tiles[:PLANES], axis=0))
-    spectrum = jnp.concatenate(parts, axis=1)
-    along = dot3(split(spectrum), (atom_h[...], atom_l[...]), ((1,), (0,)))
+    drain(3, recv_a.at[pl.ds(0, ROWS * 15)]).wait_recv()
+    along_ref[...] = along_half(lax.div(v, 2))
+    drain(4, recv_a.at[pl.ds(0, ROWS * 16)]).wait_recv()
+    along = along_ref[...] + along_half(1 - lax.div(v, 2))
 
     total = jnp.zeros((16, SLOTS), F32)
     pull_x, pull_z = total, total
@@ -501,8 +523,9 @@
             VMEM((NZ, 2 * SLOTS), BF16),
             VMEM((NZ, 2 * SLOTS), BF16),
             VMEM((NZ, 2 * SLOTS), BF16),
+            VMEM((16 * PLANES, 2 * SLOTS), F32),
             pltpu.SemaphoreType.DMA((4,)),
-            pltpu.SemaphoreType.DMA((4,)),
+            pltpu.SemaphoreType.DMA((5,)),
             pltpu.SemaphoreType.DMA((len(arrays) + 2,)),
             pltpu.SemaphoreType.REGULAR,
         ],

time: 45.4 us -> 45 us (level)
  no operation moved by 1% of the time
where the time goes in v5:
time: 45 us; the launch traced here: 44.8 us
  Pallas kernels  42.9 us (95%)
  between operations  1.93 us (4%)
    pallas_call x1, Pallas kernels, on_device(): pl.pallas_call(kernel, out_shape=jax.ShapeDtypeStruct((4, 1, 1, SLOTS), F...  42.3 us

profile of v5, /device:TPU:1, one launch (start us, length us, event | category | flops | bytes accessed | tf_op | source)
XLA Modules:
  0.0 44.8 jit_solution(14287147395779485858)
XLA Ops:
  1.9 42.3 %ewald.1.raw_ref = f32[4,1,1,512]{3,2,1,0:T(1,128)S(1)} custom-call(s32[1,1]{1,0:T(1,128)S(6)} %copy.22.count_ref, f32[1]{0:T(128)S(6)} %copy.23.factor_ref, f32[3,1,1,512]{3,2,1,0:T(1,128)} %offset_hbm.1, s32[3,1,1,512]{3,2,1,0:T(1,128)} %base_hbm.1, f32[1,1,512]{2,1,0:T(1,128)} %charge_hbm.1, bf16[512,512]{1,0:T(8,128)(2,1)} %constant.30.clone.zh_hbm, ...), custom_call_target="tpu_custom_call" | custom-call | tf_op jit(solution)/shard_map/ewald/pallas_call | solution.py:507
  44.2 0.6 %hand_out.1 = (f32[3,1,1,512]{3,2,1,0:T(1,128)}, f32[1,1,512]{2,1,0:T(1,128)}) custom-call(f32[4,1,1,512]{3,2,1,0:T(1,128)S(1)} %ewald.1.raw_ref), custom_call_target="tpu_custom_call" | custom-call | tf_op jit(solution)/shard_map/hand_out/pallas_call | solution.py:537

commit v6 on v5

--- a/solution.py
+++ b/solution.py
@@ -141,7 +141,7 @@
     def hops(offset):
         return sum(min(o, size - o) for o, size in zip(offset, sizes))
 
-    return sorted(offsets, key=lambda o: -hops(o))
+    return sorted(offsets, key=lambda o: (-hops(o), o[-1], o[0] % 2))
 
 
 def kernel(
@@ -472,9 +472,13 @@
     drain(3, recv_a.at[pl.ds(0, ROWS * 31)]).wait_send()
 
 
-def hand_out(raw_ref, force_ref, grad_ref):
-    force_ref[...] = raw_ref[0:3]
-    grad_ref[...] = raw_ref[3]
+def hand_out(raw_ref, force_hbm, grad_hbm, sems):
+    forces = pltpu.make_async_copy(raw_ref.at[pl.ds(0, 3)], force_hbm, sems.at[0])
+    grads = pltpu.make_async_copy(raw_ref.at[3], grad_hbm, sems.at[1])
+    forces.start()
+    grads.start()
+    forces.wait()
+    grads.wait()
 
 
 def on_device(offsets, bases, charges, counts, cotangent):
@@ -541,7 +545,8 @@
             jax.ShapeDtypeStruct((1, 1, SLOTS), F32),
         ),
         in_specs=[vmem],
-        out_specs=(vmem, vmem),
+        out_specs=(hbm, hbm),
+        scratch_shapes=[pltpu.SemaphoreType.DMA((2,))],
         name="hand_out",
     )(pltpu.with_memory_space_constraint(raw, VMEM))
 

time: 45 us -> 44.8 us (level)
  no operation moved by 1% of the time
where the time goes in v6:
time: 44.8 us; the launch traced here: 44.6 us
  Pallas kernels  42.7 us (95%)
  between operations  1.93 us (4%)
    pallas_call x1, Pallas kernels, on_device(): pl.pallas_call(kernel, out_shape=jax.ShapeDtypeStruct((4, 1, 1, SLOTS), F...  42 us

profile of v6, /device:TPU:1, one launch (start us, length us, event | category | flops | bytes accessed | tf_op | source)
XLA Modules:
  0.0 44.6 jit_solution(6154650033307828991)
XLA Ops:
  1.9 42.0 %ewald.1.raw_ref = f32[4,1,1,512]{3,2,1,0:T(1,128)S(1)} custom-call(s32[1,1]{1,0:T(1,128)S(6)} %copy.22.count_ref, f32[1]{0:T(128)S(6)} %copy.23.factor_ref, f32[3,1,1,512]{3,2,1,0:T(1,128)} %offset_hbm.1, s32[3,1,1,512]{3,2,1,0:T(1,128)} %base_hbm.1, f32[1,1,512]{2,1,0:T(1,128)} %charge_hbm.1, bf16[512,512]{1,0:T(8,128)(2,1)} %constant.30.clone.zh_hbm, ...), custom_call_target="tpu_custom_call" | custom-call | tf_op jit(solution)/shard_map/ewald/pallas_call | solution.py:511
  44.0 0.6 %hand_out.1 = (f32[3,1,1,512]{3,2,1,0:T(1,128)}, f32[1,1,512]{2,1,0:T(1,128)}) custom-call(f32[4,1,1,512]{3,2,1,0:T(1,128)S(1)} %ewald.1.raw_ref), custom_call_target="tpu_custom_call" | custom-call | tf_op jit(solution)/shard_map/hand_out/pallas_call | solution.py:541

commit v7 on v6

--- a/solution.py
+++ b/solution.py
@@ -197,6 +197,7 @@
     atom_h,
     atom_l,
     along_ref,
+    fold_ref,
     send_sems,
     recv_sems,
     local_sems,
@@ -328,7 +329,8 @@
     own_a = recv_a.at[pl.ds(ROWS * mine, ROWS)]
     for offset in layer:
         v_to, n_to, to = layer_mate(offset)
-        push(0, send_a.at[pl.ds(16 * (8 * v_to + n_to), ROWS)], own_a, to)
+        far = lax.rem(lax.div(v_to, 2) + lax.div(v, 2), 2)
+        push(0, send_a.at[pl.ds(16 * (8 * v_to + n_to), ROWS)], own_a, to, 5 * far)
     keep_a = pltpu.make_async_copy(send_a.at[pl.ds(16 * mine, ROWS)], own_a, local_sems.at[18])
     keep_a.start()
 
@@ -347,13 +349,18 @@
     positive = jnp.where(squared > 0.0, squared, 1.0)
     influence = jnp.where(squared > 0.0, gain_ref[...] * zfactor[1:2] / positive, 0.0)
 
+    def turn_half(which):
+        half = 8 * ROWS * 2
+        rows = recv_a[pl.ds(pl.multiple_of(half * which, 8), half), :]
+        fold_ref[which] = dot3((yth_ref[...], ytl_ref[...]), split(rows), ((1,), (0,))).T
+
     keep_a.wait()
-    drain(0, recv_a.at[pl.ds(0, ROWS * 31)]).wait_recv()
-    half = 8 * ROWS * 2
-    rows = jnp.concatenate([recv_a[:half], recv_a[half:]], axis=1)
-    columns = dot3((yth_ref[...], ytl_ref[...]), split(rows), ((1,), (0,)))
-    first = columns[:, :128].T.reshape(RING, 8, 128)
-    second = columns[:, 128:].T.reshape(RING, 8, 128)
+    drain(0, recv_a.at[pl.ds(0, ROWS * 15)]).wait_recv()
+    turn_half(lax.div(v, 2))
+    drain(5, recv_a.at[pl.ds(0, ROWS * 16)]).wait_recv()
+    turn_half(1 - lax.div(v, 2))
+    first = fold_ref[0].reshape(RING, 8, 128)
+    second = fold_ref[1].reshape(RING, 8, 128)
 
     def both(value):
         return swap(value.reshape(8 * RING, 128)).reshape(RING, 8, 128)
@@ -528,8 +535,9 @@
             VMEM((NZ, 2 * SLOTS), BF16),
             VMEM((NZ, 2 * SLOTS), BF16),
             VMEM((16 * PLANES, 2 * SLOTS), F32),
-            pltpu.SemaphoreType.DMA((4,)),
-            pltpu.SemaphoreType.DMA((5,)),
+            VMEM((2, 128, 128), F32),
+            pltpu.SemaphoreType.DMA((6,)),
+            pltpu.SemaphoreType.DMA((6,)),
             pltpu.SemaphoreType.DMA((len(arrays) + 2,)),
             pltpu.SemaphoreType.REGULAR,
         ],

time: 44.8 us -> 45.2 us (level)
  no operation moved by 1% of the time
where the time goes in v7:
time: 45.2 us; the launch traced here: 45 us
  Pallas kernels  43.1 us (95%)
  between operations  1.93 us (4%)
    pallas_call x1, Pallas kernels, on_device(): pl.pallas_call(kernel, out_shape=jax.ShapeDtypeStruct((4, 1, 1, SLOTS), F...  42.4 us

profile of v7, /device:TPU:1, one launch (start us, length us, event | category | flops | bytes accessed | tf_op | source)
XLA Modules:
  0.0 45.0 jit_solution(17260853772558715378)
XLA Ops:
  1.9 42.4 %ewald.1.raw_ref = f32[4,1,1,512]{3,2,1,0:T(1,128)S(1)} custom-call(s32[1,1]{1,0:T(1,128)S(6)} %copy.22.count_ref, f32[1]{0:T(128)S(6)} %copy.23.factor_ref, f32[3,1,1,512]{3,2,1,0:T(1,128)} %offset_hbm.1, s32[3,1,1,512]{3,2,1,0:T(1,128)} %base_hbm.1, f32[1,1,512]{2,1,0:T(1,128)} %charge_hbm.1, bf16[512,512]{1,0:T(8,128)(2,1)} %constant.30.clone.zh_hbm, ...), custom_call_target="tpu_custom_call" | custom-call | tf_op jit(solution)/shard_map/ewald/pallas_call | solution.py:518
  44.4 0.6 %hand_out.1 = (f32[3,1,1,512]{3,2,1,0:T(1,128)}, f32[1,1,512]{2,1,0:T(1,128)}) custom-call(f32[4,1,1,512]{3,2,1,0:T(1,128)S(1)} %ewald.1.raw_ref), custom_call_target="tpu_custom_call" | custom-call | tf_op jit(solution)/shard_map/hand_out/pallas_call | solution.py:549

commit v8 on v6

--- a/solution.py
+++ b/solution.py
@@ -528,8 +528,8 @@
             VMEM((NZ, 2 * SLOTS), BF16),
             VMEM((NZ, 2 * SLOTS), BF16),
             VMEM((16 * PLANES, 2 * SLOTS), F32),
-            pltpu.SemaphoreType.DMA((4,)),
-            pltpu.SemaphoreType.DMA((5,)),
+            pltpu.SemaphoreType.DMA((6,)),
+            pltpu.SemaphoreType.DMA((6,)),
             pltpu.SemaphoreType.DMA((len(arrays) + 2,)),
             pltpu.SemaphoreType.REGULAR,
         ],

time: 44.8 us -> 44.8 us (level)
  no operation moved by 1% of the time
where the time goes in v8:
time: 44.8 us; the launch traced here: 44.6 us
  Pallas kernels  42.7 us (95%)
  between operations  1.93 us (4%)
    pallas_call x1, Pallas kernels, on_device(): pl.pallas_call(kernel, out_shape=jax.ShapeDtypeStruct((4, 1, 1, SLOTS), F...  42.1 us

profile of v8, /device:TPU:1, one launch (start us, length us, event | category | flops | bytes accessed | tf_op | source)
XLA Modules:
  0.0 44.6 jit_solution(16665060730856951701)
XLA Ops:
  1.9 42.1 %ewald.1.raw_ref = f32[4,1,1,512]{3,2,1,0:T(1,128)S(1)} custom-call(s32[1,1]{1,0:T(1,128)S(6)} %copy.22.count_ref, f32[1]{0:T(128)S(6)} %copy.23.factor_ref, f32[3,1,1,512]{3,2,1,0:T(1,128)} %offset_hbm.1, s32[3,1,1,512]{3,2,1,0:T(1,128)} %base_hbm.1, f32[1,1,512]{2,1,0:T(1,128)} %charge_hbm.1, bf16[512,512]{1,0:T(8,128)(2,1)} %constant.30.clone.zh_hbm, ...), custom_call_target="tpu_custom_call" | custom-call | tf_op jit(solution)/shard_map/ewald/pallas_call | solution.py:511
  44.0 0.6 %hand_out.1 = (f32[3,1,1,512]{3,2,1,0:T(1,128)}, f32[1,1,512]{2,1,0:T(1,128)}) custom-call(f32[4,1,1,512]{3,2,1,0:T(1,128)S(1)} %ewald.1.raw_ref), custom_call_target="tpu_custom_call" | custom-call | tf_op jit(solution)/shard_map/hand_out/pallas_call | solution.py:541
